TPU v7x, 512 devices: a whole 4x4x16 slice. The times are simulated.
512 devices in a mesh: seq: 64 (over x, z_hi, y), sub: 8 (over z_lo, core).
Axes of the slice: x: 4, y: 4, z: 16 (z_hi: 4, z_lo: 4; z = z_hi * 4 + z_lo), core: 2. Of those that a mesh axis runs over, the one named last changes fastest.
Arguments:
- activation: bfloat16 [65536, 1024], P(('sub', 'seq')), may hold values from -6 to 6
- filter_raw: bfloat16 [65536, 1024], P(('sub', 'seq')), may hold values from -6 to 6
- decay_rate: float32 [1024], replicated, may hold values from 0.5 to 16
- skip_gain: float32 [1024], replicated, may hold values from 0.5 to 2
- grad_out: bfloat16 [65536, 1024], P(('sub', 'seq')), may hold values from -6 to 6
Outputs:
- grad_input: bfloat16 [65536, 1024], P(('sub', 'seq'))
- grad_raw: bfloat16 [65536, 1024], P(('sub', 'seq'))
All inputs are finite; a program needn't handle non-finite values.
Results may differ from a plain program's by a relative error of at most 0.001.
Values may be sent and summed in bfloat16 or wider, within the bound.
A program may use at most 64 MiB of HBM per device.

v0:
```python
import math

import jax
import jax.numpy as jnp
from jax import lax
from jax.sharding import PartitionSpec as P

highest = lax.Precision.HIGHEST


def angle_of(numerator, modulus):
    reduced = jnp.mod(numerator, modulus)
    return 2.0 * math.pi / modulus * reduced.astype(jnp.float32)


def complex_table(angles, inverse):
    cosine = jnp.cos(angles)
    sine = jnp.sin(angles)
    if inverse:
        return jnp.stack([jnp.stack([cosine, -sine]), jnp.stack([sine, cosine])])
    return jnp.stack([jnp.stack([cosine, sine]), jnp.stack([-sine, cosine])])


def rotate(real_part, imag_part, cosine, sine, inverse):
    if inverse:
        return jnp.stack(
            [real_part * cosine - imag_part * sine, imag_part * cosine + real_part * sine]
        )
    return jnp.stack([real_part * cosine + imag_part * sine, imag_part * cosine - real_part * sine])


def complex_mix(pattern, table, values):
    return jnp.einsum(pattern, table, values, precision=highest)


def products(spectra):
    act_spec, taps_spec, up_spec = spectra
    through_re = up_spec[0] * taps_spec[0] + up_spec[1] * taps_spec[1]
    through_im = up_spec[1] * taps_spec[0] - up_spec[0] * taps_spec[1]
    across_re = up_spec[0] * act_spec[0] + up_spec[1] * act_spec[1]
    across_im = up_spec[1] * act_spec[0] - up_spec[0] * act_spec[1]
    return jnp.stack(
        [jnp.concatenate([through_re, across_re], 0), jnp.concatenate([through_im, across_im], 0)]
    )


def per_device(activation, filter_raw, decay_rate, skip_gain, grad_out):
    tok_count, model_width = activation.shape
    seq_count = lax.axis_size("seq")
    sub_count = lax.axis_size("sub")
    dev_count = seq_count * sub_count
    seq_total = tok_count * dev_count
    length = 2 * seq_total
    chan_dev = model_width // dev_count
    seq_at = lax.axis_index("seq")
    sub_at = lax.axis_index("sub")
    freq_low = jnp.arange(2 * sub_count, dtype=jnp.int32)
    sub_rows = jnp.arange(sub_count, dtype=jnp.int32)
    seq_rows = jnp.arange(seq_count, dtype=jnp.int32)
    cell_rows = jnp.arange(tok_count, dtype=jnp.int32)
    first_angles = angle_of(freq_low[:, None] * sub_rows[None, :], 2 * sub_count)
    first_real = jnp.stack([jnp.cos(first_angles), -jnp.sin(first_angles)])
    second_angles = angle_of(seq_rows[:, None] * seq_rows[None, :], seq_count)
    second_fwd = complex_table(second_angles, False)
    second_inv = complex_table(second_angles, True)
    third_angles = angle_of(cell_rows[:, None] * cell_rows[None, :], tok_count)
    third_fwd = complex_table(third_angles, False)
    third_inv = complex_table(third_angles, True)
    low_high = freq_low[:, None] + 2 * sub_count * seq_rows[None, :]
    inner_angles = angle_of(low_high[:, :, None] * cell_rows[None, None, :], length)
    inner_cos = jnp.cos(inner_angles)
    inner_sin = jnp.sin(inner_angles)
    block_width = model_width // sub_count
    arrived = (
        lax.all_to_all(activation, "sub", split_axis=1, concat_axis=0, tiled=True),
        lax.all_to_all(filter_raw, "sub", split_axis=1, concat_axis=0, tiled=True),
        lax.all_to_all(grad_out, "sub", split_axis=1, concat_axis=0, tiled=True),
    )
    act_rows = arrived[0].reshape(sub_count, tok_count, block_width).astype(jnp.float32)
    raw_rows = arrived[1].reshape(sub_count, tok_count, block_width).astype(jnp.float32)
    up_rows = arrived[2].reshape(sub_count, tok_count, block_width).astype(jnp.float32)
    rate_part = lax.dynamic_slice_in_dim(decay_rate, sub_at * block_width, block_width)
    gain_part = lax.dynamic_slice_in_dim(skip_gain, sub_at * block_width, block_width)
    places = ((seq_count * sub_rows[:, None] + seq_at) * tok_count + cell_rows[None, :]).astype(
        jnp.float32
    )
    envelope = jnp.sqrt(2.0 * rate_part / seq_total)[None, None, :] * jnp.exp(
        -(rate_part[None, None, :] * places[:, :, None]) / seq_total
    )
    taps_rows = raw_rows * envelope
    spin_angle = angle_of(seq_at * freq_low, 2 * dev_count)[None, :, None]
    spin_cos = jnp.cos(spin_angle)
    spin_sin = jnp.sin(spin_angle)

    def spread(values):
        parts = jnp.einsum("pmb,bcd->pdmc", first_real, values, precision=highest)
        turned = rotate(parts[0], parts[1], spin_cos, spin_sin, False)
        return jnp.transpose(turned, (1, 0, 2, 3))

    gathered = (
        lax.all_to_all(spread(act_rows), "seq", split_axis=0, concat_axis=0, tiled=True),
        lax.all_to_all(spread(taps_rows), "seq", split_axis=0, concat_axis=0, tiled=True),
        lax.all_to_all(spread(up_rows), "seq", split_axis=0, concat_axis=0, tiled=True),
    )
    spectra = []
    for stacked in gathered:
        shaped = stacked.reshape(seq_count, chan_dev, 2, 2 * sub_count, tok_count)
        forward_mixed = complex_mix("pqns,sdqmc->pdmnc", second_fwd, shaped)
        forward_turned = rotate(forward_mixed[0], forward_mixed[1], inner_cos, inner_sin, False)
        spectra.append(complex_mix("pqck,qdmnc->pdmnk", third_fwd, forward_turned))
    mixed = products(spectra)
    values = mixed
    inverse_mixed = complex_mix("pqck,qdmnk->pdmnc", third_inv, values)
    inverse_turned = rotate(inverse_mixed[0], inverse_mixed[1], inner_cos, inner_sin, True)
    leaving = complex_mix("pqns,qdmnc->sdpmc", second_inv, inverse_turned)
    through = leaving[:, :chan_dev].reshape(seq_count * chan_dev, 2, 2 * sub_count, tok_count)
    across = leaving[:, chan_dev:].reshape(seq_count * chan_dev, 2, 2 * sub_count, tok_count)
    returned = (
        lax.all_to_all(through, "seq", split_axis=0, concat_axis=0, tiled=True),
        lax.all_to_all(across, "seq", split_axis=0, concat_axis=0, tiled=True),
    )
    results = []
    for stacked in returned:
        turned = rotate(stacked[:, 0], stacked[:, 1], spin_cos, spin_sin, True)
        results.append(jnp.einsum("qmb,qdmc->bcd", first_real, turned, precision=highest) / length)
    grad_input = (results[0] + gain_part[None, None, :] * up_rows).astype(jnp.bfloat16)
    grad_raw = (results[1] * envelope).astype(jnp.bfloat16)
    finished = (
        lax.all_to_all(
            grad_input.reshape(sub_count * tok_count, block_width),
            "sub",
            split_axis=0,
            concat_axis=1,
            tiled=True,
        ),
        lax.all_to_all(
            grad_raw.reshape(sub_count * tok_count, block_width),
            "sub",
            split_axis=0,
            concat_axis=1,
            tiled=True,
        ),
    )
    return (finished[0], finished[1])


def solution(mesh):
    return jax.shard_map(
        per_device,
        mesh=mesh,
        in_specs=(
            P(("sub", "seq"), None),
            P(("sub", "seq"), None),
            P(),
            P(),
            P(("sub", "seq"), None),
        ),
        out_specs=(P(("sub", "seq"), None), P(("sub", "seq"), None)),
        check_vma=False,
    )
```

profile of v0, /device:TPU:1, one launch (start us, length us, event | category | flops | bytes accessed | tf_op | source)
XLA Modules:
  0.0 626.5 jit_solution(5856540157623620073)
XLA Ops:
  2.7 10.2 %all-to-all-start = ((bf16[128,8,128]{2,0,1:T(8,128)(2,1)}), bf16[128,8,128]{2,0,1:T(8,128)(2,1)S(1)}, u32[]{:S(2)}, u32[]{:S(2)}) async-start(bf16[128,8,128]{2,0,1:T(8,128)(2,1)} %copy.129), calls=%async_computation | async-start | bytes 524288 | tf_op jit(solution)/shard_map/all_to_all | solution.py:77
  14.8 6.7 %all-to-all-done = bf16[128,8,128]{2,0,1:T(8,128)(2,1)S(1)} async-done(((bf16[128,8,128]{2,0,1:T(8,128)(2,1)}), bf16[128,8,128]{2,0,1:T(8,128)(2,1)S(1)}, u32[]{:S(2)}, u32[]{:S(2)}) %all-to-all-start) | async-done | bytes 262176 | tf_op jit(solution)/shard_map/all_to_all | solution.py:77
  21.6 4.4 all-to-all-start.4
  27.8 6.9 %all-to-all-done.4 = bf16[128,8,128]{2,0,1:T(8,128)(2,1)S(1)} async-done(((bf16[128,8,128]{2,0,1:T(8,128)(2,1)}), bf16[128,8,128]{2,0,1:T(8,128)(2,1)S(1)}, u32[]{:S(2)}, u32[]{:S(2)}) %all-to-all-start.4) | async-done | bytes 262176 | tf_op jit(solution)/shard_map/all_to_all | solution.py:75
  34.7 4.4 all-to-all-start.2
  40.1 2.4 convolution_bitcast_fusion
  42.5 5.2 all-to-all-done.2
  47.8 1.9 convolution_bitcast_fusion.2
  49.7 2.2 multiply_add_fusion.4
  52.0 2.3 copy.131
  54.3 15.5 %all-to-all-start.1 = ((f32[128,2,16,128]{3,2,1,0:T(8,128)}), f32[128,2,16,128]{3,2,1,0:T(8,128)S(1)}, u32[]{:S(2)}, u32[]{:S(2)}) async-start(f32[128,2,16,128]{3,2,1,0:T(8,128)} %copy.131), calls=%async_computation.1 | async-start | bytes 4194304 | tf_op jit(solution)/shard_map/all_to_all | solution.py:103
  69.9 3.1 maximum_bitcast_fusion.11
  72.9 3.5 copy.145
  76.4 91.4 %all-to-all-done.1 = f32[128,2,16,128]{3,2,1,0:T(8,128)S(1)} async-done(((f32[128,2,16,128]{3,2,1,0:T(8,128)}), f32[128,2,16,128]{3,2,1,0:T(8,128)S(1)}, u32[]{:S(2)}, u32[]{:S(2)}) %all-to-all-start.1) | async-done | bytes 2097184 | tf_op jit(solution)/shard_map/all_to_all | solution.py:103
  167.8 11.1 %all-to-all-start.5 = ((f32[128,2,16,128]{3,2,1,0:T(8,128)}), f32[128,2,16,128]{3,2,1,0:T(8,128)}, u32[]{:S(2)}, u32[]{:S(2)}) async-start(f32[128,2,16,128]{3,2,1,0:T(8,128)} %copy.145), calls=%async_computation.5 | async-start | bytes 4194304 | tf_op jit(solution)/shard_map/all_to_all | solution.py:101
  178.9 2.7 maximum_bitcast_fusion.8
  181.6 3.4 copy.138
  185.0 83.4 %all-to-all-done.5 = f32[128,2,16,128]{3,2,1,0:T(8,128)} async-done(((f32[128,2,16,128]{3,2,1,0:T(8,128)}), f32[128,2,16,128]{3,2,1,0:T(8,128)}, u32[]{:S(2)}, u32[]{:S(2)}) %all-to-all-start.5) | async-done | bytes 2097184 | tf_op jit(solution)/shard_map/all_to_all | solution.py:101
  268.4 17.2 %all-to-all-start.3 = ((f32[128,2,16,128]{3,2,1,0:T(8,128)}), f32[128,2,16,128]{3,2,1,0:T(8,128)}, u32[]{:S(2)}, u32[]{:S(2)}) async-start(f32[128,2,16,128]{3,2,1,0:T(8,128)} %copy.138), calls=%async_computation.3 | async-start | bytes 4194304 | tf_op jit(solution)/shard_map/all_to_all | solution.py:102
  287.9 2.1 fusion.107
  290.0 4.6 fusion.32
  294.7 4.7 fusion.38
  299.4 79.8 %all-to-all-done.3 = f32[128,2,16,128]{3,2,1,0:T(8,128)} async-done(((f32[128,2,16,128]{3,2,1,0:T(8,128)}), f32[128,2,16,128]{3,2,1,0:T(8,128)}, u32[]{:S(2)}, u32[]{:S(2)}) %all-to-all-start.3) | async-done | bytes 2097184 | tf_op jit(solution)/shard_map/all_to_all | solution.py:102
  379.3 5.2 fusion.35
  385.8 1.8 fusion.42
  387.6 1.8 fusion.43
  389.4 1.8 fusion.41
  393.9 4.1 fusion.5
  399.1 3.9 fusion.8
  403.0 1.8 fusion.163
  404.8 2.6 copy.154
  407.4 34.7 %all-to-all-start.6 = ((f32[128,2,16,128]{3,2,1,0:T(8,128)}), f32[128,2,16,128]{3,2,1,0:T(8,128)S(1)}, u32[]{:S(2)}, u32[]{:S(2)}) async-start(f32[128,2,16,128]{3,2,1,0:T(8,128)} %bitcast.278), calls=%async_computation.6 | async-start | bytes 4194304 | tf_op jit(solution)/shard_map/all_to_all | solution.py:119
  442.0 4.2 copy.159
  446.2 63.5 %all-to-all-done.6 = f32[128,2,16,128]{3,2,1,0:T(8,128)S(1)} async-done(((f32[128,2,16,128]{3,2,1,0:T(8,128)}), f32[128,2,16,128]{3,2,1,0:T(8,128)S(1)}, u32[]{:S(2)}, u32[]{:S(2)}) %all-to-all-start.6) | async-done | bytes 2097184 | tf_op jit(solution)/shard_map/all_to_all | solution.py:119
  509.7 1.3 copy-done.2
  511.1 9.6 %all-to-all-start.8 = ((f32[128,2,16,128]{3,2,1,0:T(8,128)}), f32[128,2,16,128]{3,2,1,0:T(8,128)S(1)}, u32[]{:S(2)}, u32[]{:S(2)}) async-start(f32[128,2,16,128]{3,2,1,0:T(8,128)} %bitcast.277), calls=%async_computation.8 | async-start | bytes 4194304 | tf_op jit(solution)/shard_map/all_to_all | solution.py:120
  520.7 3.1 fusion.165
  523.8 1.8 copy.199
  525.6 2.8 copy.200
  528.4 60.7 %all-to-all-done.8 = f32[128,2,16,128]{3,2,1,0:T(8,128)S(1)} async-done(((f32[128,2,16,128]{3,2,1,0:T(8,128)}), f32[128,2,16,128]{3,2,1,0:T(8,128)S(1)}, u32[]{:S(2)}, u32[]{:S(2)}) %all-to-all-start.8) | async-done | bytes 2097184 | tf_op jit(solution)/shard_map/all_to_all | solution.py:120
  589.1 1.5 fusion.164
  590.5 2.9 copy.201
  593.4 1.6 copy.202
  595.0 2.4 fusion.74
  599.4 4.1 all-to-all-start.9
  606.3 6.0 all-to-all-done.9
  612.2 4.4 all-to-all-start.7
  617.6 7.7 %all-to-all-done.7 = bf16[8,128,128]{2,1,0:T(8,128)(2,1)S(1)} async-done(((bf16[8,128,128]{2,1,0:T(8,128)(2,1)}), bf16[8,128,128]{2,1,0:T(8,128)(2,1)S(1)}, u32[]{:S(2)}, u32[]{:S(2)}) %all-to-all-start.7) | async-done | bytes 262176 | tf_op jit(solution)/shard_map/all_to_all | solution.py:129
  (71 shorter events, 21.0 us)
Async XLA Ops:
  0.6 25.3 %copy-start.13 = (bf16[128,1024]{1,0:T(8,128)(2,1)S(1)}, bf16[128,1024]{1,0:T(8,128)(2,1)}, u32[]{:S(2)}) copy-start(bf16[128,1024]{1,0:T(8,128)(2,1)} %param.6) | copy-start | bytes 786436
  2.7 18.9 %all-to-all-start = ((bf16[128,8,128]{2,0,1:T(8,128)(2,1)}), bf16[128,8,128]{2,0,1:T(8,128)(2,1)S(1)}, u32[]{:S(2)}, u32[]{:S(2)}) async-start(bf16[128,8,128]{2,0,1:T(8,128)(2,1)} %copy.129), calls=%async_computation | async-start | bytes 524288 | tf_op jit(solution)/shard_map/all_to_all | solution.py:77
  21.6 13.1 %all-to-all-start.4 = ((bf16[128,8,128]{2,0,1:T(8,128)(2,1)}), bf16[128,8,128]{2,0,1:T(8,128)(2,1)S(1)}, u32[]{:S(2)}, u32[]{:S(2)}) async-start(bf16[128,8,128]{2,0,1:T(8,128)(2,1)} %copy.143), calls=%async_computation.4 | async-start | bytes 524288 | tf_op jit(solution)/shard_map/all_to_all | solution.py:75
  27.8 20.0 %copy-start.14 = (f32[128]{0:T(128)}, f32[128]{0:T(128)S(1)}, u32[]{:S(2)}) copy-start(f32[128]{0:T(128)S(1)} %get-tuple-element.6) | copy-start | bytes 1540
  27.8 20.0 %copy-start.16 = (f32[128]{0:T(128)}, f32[128]{0:T(128)S(1)}, u32[]{:S(2)}) copy-start(f32[128]{0:T(128)S(1)} %get-tuple-element.7) | copy-start | bytes 1540
  34.7 13.1 %all-to-all-start.2 = ((bf16[128,8,128]{2,0,1:T(8,128)(2,1)}), bf16[128,8,128]{2,0,1:T(8,128)(2,1)S(1)}, u32[]{:S(2)}, u32[]{:S(2)}) async-start(bf16[128,8,128]{2,0,1:T(8,128)(2,1)} %copy.135), calls=%async_computation.2 | async-start | bytes 524288 | tf_op jit(solution)/shard_map/all_to_all | solution.py:76
  39.1 8.7 %copy-start.11 = (f32[8,128]{0,1:T(8,128)}, f32[8,128]{0,1:T(8,128)S(1)}, u32[]{:S(2)}) copy-start(f32[8,128]{0,1:T(8,128)S(1)} %add_convert_fusion) | copy-start | bytes 12292
  47.7 1.9 copy-start
  54.3 113.5 %all-to-all-start.1 = ((f32[128,2,16,128]{3,2,1,0:T(8,128)}), f32[128,2,16,128]{3,2,1,0:T(8,128)S(1)}, u32[]{:S(2)}, u32[]{:S(2)}) async-start(f32[128,2,16,128]{3,2,1,0:T(8,128)} %copy.131), calls=%async_computation.1 | async-start | bytes 4194304 | tf_op jit(solution)/shard_map/all_to_all | solution.py:103
  167.8 100.6 %all-to-all-start.5 = ((f32[128,2,16,128]{3,2,1,0:T(8,128)}), f32[128,2,16,128]{3,2,1,0:T(8,128)}, u32[]{:S(2)}, u32[]{:S(2)}) async-start(f32[128,2,16,128]{3,2,1,0:T(8,128)} %copy.145), calls=%async_computation.5 | async-start | bytes 4194304 | tf_op jit(solution)/shard_map/all_to_all | solution.py:101
  268.4 110.8 %all-to-all-start.3 = ((f32[128,2,16,128]{3,2,1,0:T(8,128)}), f32[128,2,16,128]{3,2,1,0:T(8,128)}, u32[]{:S(2)}, u32[]{:S(2)}) async-start(f32[128,2,16,128]{3,2,1,0:T(8,128)} %copy.138), calls=%async_computation.3 | async-start | bytes 4194304 | tf_op jit(solution)/shard_map/all_to_all | solution.py:102
  287.1 7.5 %copy-start.5 = (f32[1,2,64,64]{3,2,1,0:T(8,128)}, f32[1,2,64,64]{3,2,1,0:T(8,128)S(1)}, u32[]{:S(2)}) copy-start(f32[1,2,64,64]{3,2,1,0:T(8,128)S(1)} %get-tuple-element.44) | copy-start | bytes 98308
  287.1 7.5 %copy-start.6 = (f32[1,2,64,64]{3,2,1,0:T(8,128)}, f32[1,2,64,64]{3,2,1,0:T(8,128)S(1)}, u32[]{:S(2)}) copy-start(f32[1,2,64,64]{3,2,1,0:T(8,128)S(1)} %get-tuple-element.49) | copy-start | bytes 98308
  379.3 5.2 copy-start.1
  384.5 1.3 copy-start.4
  392.9 0.9 copy-start.7
  392.9 1.0 copy-start.8
  398.0 1.0 copy-start.9
  398.1 1.0 copy-start.10
  407.4 102.4 %all-to-all-start.6 = ((f32[128,2,16,128]{3,2,1,0:T(8,128)}), f32[128,2,16,128]{3,2,1,0:T(8,128)S(1)}, u32[]{:S(2)}, u32[]{:S(2)}) async-start(f32[128,2,16,128]{3,2,1,0:T(8,128)} %bitcast.278), calls=%async_computation.6 | async-start | bytes 4194304 | tf_op jit(solution)/shard_map/all_to_all | solution.py:119
  509.7 1.3 copy-start.2
  511.1 78.0 %all-to-all-start.8 = ((f32[128,2,16,128]{3,2,1,0:T(8,128)}), f32[128,2,16,128]{3,2,1,0:T(8,128)S(1)}, u32[]{:S(2)}, u32[]{:S(2)}) async-start(f32[128,2,16,128]{3,2,1,0:T(8,128)} %bitcast.277), calls=%async_computation.8 | async-start | bytes 4194304 | tf_op jit(solution)/shard_map/all_to_all | solution.py:120
  590.5 2.9 copy-start.3
  595.0 2.4 copy-start.12
  595.0 2.4 copy-start.15
  595.0 2.4 copy-start.17
  599.4 12.8 %all-to-all-start.9 = ((bf16[8,128,128]{2,1,0:T(8,128)(2,1)}), bf16[8,128,128]{2,1,0:T(8,128)(2,1)S(1)}, u32[]{:S(2)}, u32[]{:S(2)}) async-start(bf16[8,128,128]{2,1,0:T(8,128)(2,1)} %copy.162), calls=%async_computation.9 | async-start | bytes 524288 | tf_op jit(solution)/shard_map/all_to_all | solution.py:136
  612.2 13.1 %all-to-all-start.7 = ((bf16[8,128,128]{2,1,0:T(8,128)(2,1)}), bf16[8,128,128]{2,1,0:T(8,128)(2,1)S(1)}, u32[]{:S(2)}, u32[]{:S(2)}) async-start(bf16[8,128,128]{2,1,0:T(8,128)(2,1)} %copy.157), calls=%async_computation.7 | async-start | bytes 524288 | tf_op jit(solution)/shard_map/all_to_all | solution.py:129
where the time goes:
time: 637 us; the launch traced here: 627 us
  waiting for transfers between devices  411 us (65%)
  starting transfers between devices  115 us (18%)
  local copies, waits for them, and re-layouts  42.9 us (7%)
  matrix products  35.8 us (6%)
  other arithmetic  19.8 us (3%)
    all_to_all x1, waiting for transfers between devices, per_device(): lax.all_to_all(spread(up_rows), 'seq', split_axis=0, concat_axis=0, tiled...  91.4 us
    all_to_all x1, waiting for transfers between devices, per_device(): lax.all_to_all(spread(act_rows), 'seq', split_axis=0, concat_axis=0, tile...  83.4 us
    all_to_all x1, waiting for transfers between devices, per_device(): lax.all_to_all(spread(taps_rows), 'seq', split_axis=0, concat_axis=0, til...  79.8 us
    all_to_all x1, waiting for transfers between devices, per_device(): lax.all_to_all(through, 'seq', split_axis=0, concat_axis=0, tiled=True)  63.5 us
    all_to_all x1, waiting for transfers between devices, per_device(): lax.all_to_all(across, 'seq', split_axis=0, concat_axis=0, tiled=True)  60.7 us
    all_to_all x1, starting transfers between devices, per_device(): lax.all_to_all(through, 'seq', split_axis=0, concat_axis=0, tiled=True)  34.7 us
    dot_general x8, matrix products, complex_mix(): return jnp.einsum(pattern, table, values, precision=highest)  28 us
    all_to_all x1, starting transfers between devices, per_device(): lax.all_to_all(spread(taps_rows), 'seq', split_axis=0, concat_axis=0, til...  17.2 us
  transfers between devices with their start and end apart: 10, of which 10 were waited for; matrix products, arithmetic and copies ran while one was open for 8% of the time, Pallas kernels for 0%

commit v1 on v0

v1 whole, which is shorter than its diff:
```python
import functools
import math

import jax
import jax.numpy as jnp
from jax import lax
from jax.experimental import pallas as pl
from jax.experimental.pallas import tpu as pltpu
from jax.sharding import PartitionSpec as P

both = ("sub", "seq")
two_stage = True


def split_halves(values):
    high = lax.reduce_precision(values, 8, 7)
    return high.astype(jnp.bfloat16), (values - high).astype(jnp.bfloat16)


def halves(values):
    high = values.astype(jnp.bfloat16)
    return high, (values - high.astype(jnp.float32)).astype(jnp.bfloat16)


def mul(left, right):
    return jnp.dot(left, right, preferred_element_type=jnp.float32)


def mul3(left, right):
    left_hi, left_lo = left
    right_hi, right_lo = right
    return mul(left_hi, right_hi) + (mul(left_hi, right_lo) + mul(left_lo, right_hi))


def correlate(
    chan, cell, chunk, scale,
    got_ref, env_ref, gain_ref, fwd_hi_ref, fwd_lo_ref, back_hi_ref, back_lo_ref,
    inner_hi_ref, inner_lo_ref, outer_hi_ref, outer_lo_ref, cos_ref, sin_ref,
    out_ref, taps_hi_ref, taps_lo_ref, total_ref,
):
    step = pl.program_id(0)
    width = chan * cell

    @pl.when(step == 0)
    def _():
        taps = got_ref[:, width : 2 * width].astype(jnp.float32) * env_ref[...]
        high, low = halves(taps)
        taps_hi_ref[...] = high
        taps_lo_ref[...] = low
        total_ref[...] = jnp.zeros_like(total_ref)

    fwd_hi = fwd_hi_ref[...]
    fwd_lo = fwd_lo_ref[...]
    act = got_ref[:, 0:width]
    up = got_ref[:, 2 * width : 3 * width]
    first = (
        mul(fwd_hi, act) + mul(fwd_lo, act),
        mul(fwd_hi, taps_hi_ref[...])
        + (mul(fwd_hi, taps_lo_ref[...]) + mul(fwd_lo, taps_hi_ref[...])),
        mul(fwd_hi, up) + mul(fwd_lo, up),
    )
    cosine = cos_ref[...]
    sine = sin_ref[...]
    inner = (inner_hi_ref[...], inner_lo_ref[...])
    outer = (outer_hi_ref[...], outer_lo_ref[...])
    spectra = []
    for values in first:
        rows = []
        for c in range(chan):
            re = values[:chunk, c * cell : (c + 1) * cell]
            im = values[chunk:, c * cell : (c + 1) * cell]
            rows.append(
                jnp.concatenate([re * cosine + im * sine, im * cosine - re * sine], axis=1)
            )
        spectra.append(mul3(halves(jnp.concatenate(rows, axis=0)), inner))
    up_re, up_im = spectra[2][:, :cell], spectra[2][:, cell:]
    parts_re, parts_im = [], []
    for other in (spectra[1], spectra[0]):
        re, im = other[:, :cell], other[:, cell:]
        mixed = jnp.concatenate([up_re * re + up_im * im, up_im * re - up_re * im], axis=1)
        back = mul3(halves(mixed), outer)
        for c in range(chan):
            zre = back[c * chunk : (c + 1) * chunk, :cell]
            zim = back[c * chunk : (c + 1) * chunk, cell:]
            parts_re.append(zre * cosine - zim * sine)
            parts_im.append(zim * cosine + zre * sine)
    spread = jnp.concatenate(
        [jnp.concatenate(parts_re, axis=1), jnp.concatenate(parts_im, axis=1)], axis=0
    )
    total_ref[...] += mul3((back_hi_ref[...], back_lo_ref[...]), halves(spread))

    @pl.when(step == pl.num_programs(0) - 1)
    def _():
        through = total_ref[:, :width] * scale
        across = total_ref[:, width:] * scale
        up_float = got_ref[:, 2 * width : 3 * width].astype(jnp.float32)
        out_ref[:, :width] = (through + gain_ref[...] * up_float).astype(jnp.bfloat16)
        out_ref[:, width:] = (across * env_ref[...]).astype(jnp.bfloat16)


def local_part(got, rate, gain, places, chan, cell, total_tokens, interpret=False):
    blocks = got.shape[0]
    chunk = min(128, blocks)
    steps = blocks // chunk
    length = 2 * total_tokens
    width = chan * cell
    freq = jnp.arange(blocks, dtype=jnp.int32)
    odd = 2 * freq + 1

    def angle(numerator, modulus):
        return (2.0 * math.pi / modulus) * (numerator % modulus).astype(jnp.float32)

    fwd_angle = angle(odd[:, None] * places[None, :], 4 * blocks).reshape(steps, 1, chunk, blocks)
    fwd = jnp.concatenate([jnp.cos(fwd_angle), -jnp.sin(fwd_angle)], 1)
    fwd_hi, fwd_lo = split_halves(fwd.reshape(2 * blocks, blocks))
    back_angle = angle(places[:, None] * odd[None, :], 4 * blocks).reshape(blocks, steps, 1, chunk)
    back = jnp.concatenate([jnp.cos(back_angle), -jnp.sin(back_angle)], 2)
    back_hi, back_lo = split_halves(back.reshape(blocks, 2 * blocks))
    cells = jnp.arange(cell, dtype=jnp.int32)
    inner_angle = angle(cells[:, None] * cells[None, :], cell)
    icos, isin = jnp.cos(inner_angle), jnp.sin(inner_angle)
    inner = jnp.concatenate(
        [jnp.concatenate([icos, -isin], 1), jnp.concatenate([isin, icos], 1)], 0
    )
    outer = jnp.concatenate(
        [jnp.concatenate([icos, isin], 1), jnp.concatenate([-isin, icos], 1)], 0
    )
    inner_hi, inner_lo = split_halves(inner)
    outer_hi, outer_lo = split_halves(outer)
    turn = angle(odd[:, None] * cells[None, :], 2 * length)
    at = (places[:, None] * cell + cells[None, :]).astype(jnp.float32)
    env = jnp.concatenate(
        [
            jnp.sqrt(2.0 * rate[c] / total_tokens) * jnp.exp(-(rate[c] * at) / total_tokens)
            for c in range(chan)
        ],
        1,
    )
    gain_row = jnp.repeat(gain, cell)[None, :]
    whole = lambda shape: pl.BlockSpec(shape, lambda i: (0, 0))
    flops = 2 * 3 * (5 * 2 * blocks * blocks * width + 5 * chan * blocks * 4 * cell * cell)
    return pl.pallas_call(
        functools.partial(correlate, chan, cell, chunk, 2.0 / length),
        grid=(steps,),
        out_shape=jax.ShapeDtypeStruct((blocks, 2 * width), jnp.bfloat16),
        in_specs=[
            whole((blocks, 3 * width)),
            whole((blocks, width)),
            whole((1, width)),
            pl.BlockSpec((2 * chunk, blocks), lambda i: (i, 0)),
            pl.BlockSpec((2 * chunk, blocks), lambda i: (i, 0)),
            pl.BlockSpec((blocks, 2 * chunk), lambda i: (0, i)),
            pl.BlockSpec((blocks, 2 * chunk), lambda i: (0, i)),
            whole((2 * cell, 2 * cell)),
            whole((2 * cell, 2 * cell)),
            whole((2 * cell, 2 * cell)),
            whole((2 * cell, 2 * cell)),
            pl.BlockSpec((chunk, cell), lambda i: (i, 0)),
            pl.BlockSpec((chunk, cell), lambda i: (i, 0)),
        ],
        out_specs=whole((blocks, 2 * width)),
        scratch_shapes=[
            pltpu.VMEM((blocks, width), jnp.bfloat16),
            pltpu.VMEM((blocks, width), jnp.bfloat16),
            pltpu.VMEM((blocks, 2 * width), jnp.float32),
        ],
        cost_estimate=pl.CostEstimate(flops=flops, bytes_accessed=8 * 2**20, transcendentals=0),
        interpret=interpret,
    )(
        got, env, gain_row, fwd_hi, fwd_lo, back_hi, back_lo,
        inner_hi, inner_lo, outer_hi, outer_lo, jnp.cos(turn), jnp.sin(turn),
    )


def per_device(activation, filter_raw, decay_rate, skip_gain, grad_out, interpret=False):
    cell, model_width = activation.shape
    seq_count = lax.axis_size("seq")
    sub_count = lax.axis_size("sub")
    blocks = seq_count * sub_count
    chan = model_width // blocks
    seq_at = lax.axis_index("seq")
    sub_at = lax.axis_index("sub")
    leaving = jnp.stack(
        [jnp.transpose(v).reshape(blocks, chan, cell) for v in (activation, filter_raw, grad_out)],
        axis=1,
    )
    row = jnp.arange(blocks, dtype=jnp.int32)
    if two_stage:
        leaving = leaving.reshape(sub_count, seq_count, 3, chan, cell)
        near = lax.all_to_all(leaving, "sub", 0, 0)
        near = jnp.transpose(near, (1, 0, 2, 3, 4))
        got = lax.all_to_all(near, "seq", 0, 0).reshape(blocks, 3 * chan * cell)
        places = (row % sub_count) * seq_count + row // sub_count
    else:
        got = lax.all_to_all(leaving, both, 0, 0).reshape(blocks, 3 * chan * cell)
        places = row
    first_chan = (sub_at * seq_count + seq_at) * chan
    rate = lax.dynamic_slice_in_dim(decay_rate, first_chan, chan)
    gain = lax.dynamic_slice_in_dim(skip_gain, first_chan, chan)
    done = local_part(got, rate, gain, places, chan, cell, blocks * cell, interpret)
    if two_stage:
        done = done.reshape(seq_count, sub_count, 2, chan, cell)
        far = jnp.transpose(lax.all_to_all(done, "seq", 0, 0), (1, 0, 2, 3, 4))
        back = lax.all_to_all(far, "sub", 0, 0)
    else:
        back = lax.all_to_all(done.reshape(blocks, 2, chan, cell), both, 0, 0)
    back = back.reshape(blocks, 2, chan, cell)
    return tuple(
        jnp.transpose(back[:, o].reshape(model_width, cell)) for o in range(2)
    )


def solution(mesh, interpret=False):
    return jax.shard_map(
        functools.partial(per_device, interpret=interpret),
        mesh=mesh,
        in_specs=(P(both, None), P(both, None), P(), P(), P(both, None)),
        out_specs=(P(both, None), P(both, None)),
        check_vma=False,
    )
```

time: 637 us -> 171 us (0.27); the launches traced: 627 us -> 171 us
  waiting for transfers between devices: 411 us -> 13.5 us
  starting transfers between devices: 115 us -> 16.1 us
  blocking collectives: 0 us -> 90.9 us
  matrix products: 35.8 us -> 0 us
  local copies, waits for them, and re-layouts: 42.9 us -> 17.9 us
  Pallas kernels: 0 us -> 11.1 us
    all_to_all x10 -> x1, waiting for transfers between devices: 411 us -> 13.5 us  [per_device(): got = lax.all_to_all(near, 'seq', 0, 0).reshape(blocks, 3 * chan * cell)]
    all_to_all x10 -> x1, starting transfers between devices: 115 us -> 16.1 us  [per_device(): got = lax.all_to_all(near, 'seq', 0, 0).reshape(blocks, 3 * chan * cell)]
    all_to_all x0 -> x3, blocking collectives: none -> 90.9 us  [the longest x1 42.9 us: per_device(): far = jnp.transpose(lax.all_to_all(done, 'seq', 0, 0), (1, 0, 2, 3, 4))]
    dot_general x13 -> x0, matrix products: 35.8 us -> none  [the longest x8 28 us: complex_mix(): return jnp.einsum(pattern, table, values, precision=highest)]
    slice x5 -> x4, local copies, waits for them, and re-layouts: 13.1 us -> 1.16 us  [the longest x1 0.58 us: local_part(): rate[c]]
    pallas_call x0 -> x1, Pallas kernels: none -> 11.1 us  [local_part(): pl.pallas_call(functools.partial(correlate, chan, cell, chunk, 2.0 / leng...]
    unnamed x45 -> x5, local copies, waits for them, and re-layouts: 15.5 us -> 5.06 us
    transpose x3 -> x2, local copies, waits for them, and re-layouts: 9.16 us -> 1.62 us  [the longest x1 1.42 us: per_device(): near = jnp.transpose(near, (1, 0, 2, 3, 4))]
  transfers between devices with their start and end apart: 10 -> 1, of which waited for: 10 -> 1; matrix products, arithmetic and copies ran while one was open for 8% -> 15% of each run, Pallas kernels for 0% -> 0%
where the time goes in v1:
time: 171 us
  blocking collectives  90.9 us (53%)
  other arithmetic  19 us (11%)
  local copies, waits for them, and re-layouts  17.9 us (10%)
  starting transfers between devices  16.1 us (9%)
  waiting for transfers between devices  13.5 us (8%)
  Pallas kernels  11.1 us (6%)
  between operations  2.16 us (1%)
    all_to_all x1, blocking collectives, per_device(): far = jnp.transpose(lax.all_to_all(done, 'seq', 0, 0), (1, 0, 2, 3, 4))  42.9 us
    all_to_all x1, blocking collectives, per_device(): near = lax.all_to_all(leaving, 'sub', 0, 0)  29.2 us
    all_to_all x1, blocking collectives, per_device(): back = lax.all_to_all(far, 'sub', 0, 0)  18.8 us
    all_to_all x1, starting transfers between devices, per_device(): got = lax.all_to_all(near, 'seq', 0, 0).reshape(blocks, 3 * chan * cell)  16.1 us
    all_to_all x1, waiting for transfers between devices, per_device(): got = lax.all_to_all(near, 'seq', 0, 0).reshape(blocks, 3 * chan * cell)  13.5 us
    pallas_call x1, Pallas kernels, local_part(): pl.pallas_call(functools.partial(correlate, chan, cell, chunk, 2.0 / leng...  11.1 us
    unnamed x5, local copies, waits for them, and re-layouts  5.06 us
    convert_element_type x3, other arithmetic, split_halves(): return (high.astype(jnp.bfloat16), (values - high).astype(jnp.bfloat16))  4.23 us
  transfers between devices with their start and end apart: 1, of which 1 were waited for; matrix products, arithmetic and copies ran while one was open for 15% of the time, Pallas kernels for 0%

profile of v1, /device:TPU:1, one launch (start us, length us, event | category | flops | bytes accessed | tf_op | source)
XLA Modules:
  0.0 170.7 jit_solution(11878110234334495345)
XLA Ops:
  0.6 1.1 copy.31
  1.8 1.1 copy.32
  2.9 1.1 copy.33
  4.0 1.3 pad_maximum_fusion.2
  5.3 0.8 copy.34
  6.1 29.2 %all_to_all.20 = bf16[8,64,3,2,128]{4,3,1,2,0:T(2,128)(2,1)S(1)} all-to-all(bf16[8,64,3,2,128]{4,3,1,2,0:T(2,128)(2,1)S(1)} %copy.34), channel_id=1, replica_groups=mesh['seq'=64,'sub'=8] {'sub'}, dimensions={0} | all-to-all | bytes 1572864 | tf_op jit(solution)/shard_map/all_to_all | solution.py:190
  35.4 1.4 copy.35
  36.8 16.1 %all-to-all-start.1 = ((bf16[64,8,3,2,128]{4,3,1,2,0:T(2,128)(2,1)}), bf16[64,8,3,2,128]{4,3,1,2,0:T(2,128)(2,1)S(1)}, u32[]{:S(2)}, u32[]{:S(2)}) async-start(bf16[64,8,3,2,128]{4,3,1,2,0:T(2,128)(2,1)} %copy.35), calls=%async_computation.1 | async-start | bytes 1572864 | tf_op jit(solution)/shard_map/all_to_all | solution.py:192
  52.9 0.8 dynamic_slice.6
  53.7 0.6 fusion.41
  55.7 0.8 dynamic_slice.7
  56.4 4.2 %fusion.8 = (f32[512,4,1,128]{3,0,2,1:T(8,128)S(1)}, f32[512,4,1,128]{3,0,2,1:T(8,128)S(1)}) fusion(s32[4,128]{1,0:T(4,128)S(1)} %multiply_add_fusion.1, s32[512]{0:T(512)S(1)} %fusion.35), kind=kLoop, calls=%fused_computation.28 | loop fusion | flops 3932160 | bytes 2101248 | tf_op jit(solution)/shard_map/cos | solution.py:117
  60.6 0.1 pad_maximum_fusion.1
  60.8 2.9 %copy.37 = f32[512,4,2,128]{3,2,1,0:T(2,128)} copy(f32[512,4,2,128]{3,0,2,1:T(8,128)S(1)} %pad_maximum_fusion.1) | data formatting | bytes 4194304 | tf_op jit(solution)/shard_map/concatenate | solution.py:117
  63.7 3.1 %reshape.245 = f32[512,1024]{1,0:T(8,128)S(1)} reshape(f32[512,4,2,128]{3,2,1,0:T(2,128)} %copy.37) | data formatting | bytes 4194304 | tf_op jit(solution)/shard_map/reshape | solution.py:118
  66.9 0.3 fusion.30
  67.1 0.3 fusion.28
  67.4 1.5 exponential_multiply_fusion.1
  68.9 0.8 pad_maximum_fusion.3.env_ref
  69.7 0.8 fusion.13
  70.5 4.2 %fusion.9 = (f32[4,1,128,512]{3,2,1,0:T(8,128)S(1)}, f32[4,1,128,512]{3,2,1,0:T(8,128)S(1)}) fusion(s32[512]{0:T(512)S(1)} %fusion.35, s32[4,128]{1,0:T(4,128)S(1)} %multiply_add_fusion.1), kind=kLoop, calls=%fused_computation.29 | loop fusion | flops 3932160 | bytes 2101248 | tf_op jit(solution)/shard_map/cos | solution.py:114
  74.7 0.2 pad_maximum_fusion
  74.9 1.9 %fusion.20 = (f32[512,128]{1,0:T(8,128)}, f32[512,128]{1,0:T(8,128)}) fusion(s32[512]{0:T(512)S(1)} %multiply_add_fusion), kind=kLoop, calls=%fused_computation.54 | loop fusion | flops 917504 | bytes 526336 | tf_op jit(solution)/shard_map/sin | solution.py:171
  76.9 1.8 %fusion.1 = (bf16[512,1024]{1,0:T(8,128)(2,1)}, bf16[512,1024]{1,0:T(8,128)(2,1)}) fusion(f32[512,1024]{1,0:T(8,128)S(1)} %reshape.245), kind=kLoop, calls=%fused_computation.5 | loop fusion | flops 2097152 | bytes 4194304 | tf_op jit(solution)/shard_map/convert_element_type | solution.py:17
  78.6 1.6 fusion
  80.3 13.5 %all-to-all-done.1 = bf16[64,8,3,2,128]{4,3,1,2,0:T(2,128)(2,1)S(1)} async-done(((bf16[64,8,3,2,128]{4,3,1,2,0:T(2,128)(2,1)}), bf16[64,8,3,2,128]{4,3,1,2,0:T(2,128)(2,1)S(1)}, u32[]{:S(2)}, u32[]{:S(2)}) %all-to-all-start.1) | async-done | bytes 786464 | tf_op jit(solution)/shard_map/all_to_all | solution.py:192
  93.8 1.0 copy.36
  94.8 0.6 broadcast_in_dim.2
  95.4 11.1 %shard_map.68 = bf16[512,512]{1,0:T(8,128)(2,1)} custom-call(bf16[512,768]{1,0:T(8,128)(2,1)} %bitcast.34, f32[512,256]{1,0:T(8,128)} %pad_maximum_fusion.3.env_ref, f32[1,256]{1,0:T(1,128)} %bitcast.36, bf16[1024,512]{1,0:T(8,128)(2,1)} %get-tuple-element.11.fwd_hi_ref, bf16[1024,512]{1,0:T(8,128)(2,1)} %get-tuple-element.10.fwd_lo_ref, ...), custom_call_target="tpu_custom_call" | custom-call | flops 6039797760 | bytes 8388608 | tf_op jit(solution)/shard_map/pallas_call | solution.py:142
  106.5 42.9 %all_to_all.21 = bf16[64,8,2,2,128]{4,1,3,2,0:T(8,128)(2,1)S(1)} all-to-all(bf16[64,8,2,2,128]{4,1,3,2,0:T(8,128)(2,1)} %bitcast.35), channel_id=1, replica_groups=mesh['seq'=64,'sub'=8] {'seq'}, dimensions={0} | all-to-all | bytes 1048576 | tf_op jit(solution)/shard_map/all_to_all | solution.py:203
  149.3 0.2 copy.38
  149.5 18.8 %all_to_all.22 = bf16[8,64,2,2,128]{4,1,3,2,0:T(8,128)(2,1)S(1)} all-to-all(bf16[8,64,2,2,128]{4,1,3,2,0:T(8,128)(2,1)S(1)} %copy.38), channel_id=1, replica_groups=mesh['seq'=64,'sub'=8] {'sub'}, dimensions={0} | all-to-all | bytes 1048576 | tf_op jit(solution)/shard_map/all_to_all | solution.py:204
  168.4 0.3 copy.40
  168.7 0.9 copy.42
  169.5 0.3 copy.41
  169.8 0.9 copy.43
  (6 shorter events, 0.1 us)
Async XLA Ops:
  36.8 57.0 %all-to-all-start.1 = ((bf16[64,8,3,2,128]{4,3,1,2,0:T(2,128)(2,1)}), bf16[64,8,3,2,128]{4,3,1,2,0:T(2,128)(2,1)S(1)}, u32[]{:S(2)}, u32[]{:S(2)}) async-start(bf16[64,8,3,2,128]{4,3,1,2,0:T(2,128)(2,1)} %copy.35), calls=%async_computation.1 | async-start | bytes 1572864 | tf_op jit(solution)/shard_map/all_to_all | solution.py:192

commit v2 on v1

--- a/solution.py
+++ b/solution.py
@@ -8,8 +8,9 @@
 from jax.experimental.pallas import tpu as pltpu
 from jax.sharding import PartitionSpec as P
 
-both = ("sub", "seq")
-two_stage = True
+tokens_over = ("zl", "core", "x", "zh", "y")
+plane = ("x", "y", "core")
+ring = ("zh", "zl")
 
 
 def split_halves(values):
@@ -174,47 +175,45 @@
 
 def per_device(activation, filter_raw, decay_rate, skip_gain, grad_out, interpret=False):
     cell, model_width = activation.shape
-    seq_count = lax.axis_size("seq")
-    sub_count = lax.axis_size("sub")
-    blocks = seq_count * sub_count
+    nx, nzh, ny, nzl, ncore = (lax.axis_size(n) for n in ("x", "zh", "y", "zl", "core"))
+    flat = nx * ny * ncore
+    deep = nzh * nzl
+    blocks = flat * deep
     chan = model_width // blocks
-    seq_at = lax.axis_index("seq")
-    sub_at = lax.axis_index("sub")
     leaving = jnp.stack(
-        [jnp.transpose(v).reshape(blocks, chan, cell) for v in (activation, filter_raw, grad_out)],
-        axis=1,
-    )
+        [
+            jnp.transpose(v).reshape(flat, deep, chan, cell)
+            for v in (activation, filter_raw, grad_out)
+        ],
+        axis=2,
+    )
+    near = jnp.transpose(lax.all_to_all(leaving, plane, 0, 0), (1, 0, 2, 3, 4))
+    got = lax.all_to_all(near, ring, 0, 0).reshape(blocks, 3 * chan * cell)
     row = jnp.arange(blocks, dtype=jnp.int32)
-    if two_stage:
-        leaving = leaving.reshape(sub_count, seq_count, 3, chan, cell)
-        near = lax.all_to_all(leaving, "sub", 0, 0)
-        near = jnp.transpose(near, (1, 0, 2, 3, 4))
-        got = lax.all_to_all(near, "seq", 0, 0).reshape(blocks, 3 * chan * cell)
-        places = (row % sub_count) * seq_count + row // sub_count
-    else:
-        got = lax.all_to_all(leaving, both, 0, 0).reshape(blocks, 3 * chan * cell)
-        places = row
-    first_chan = (sub_at * seq_count + seq_at) * chan
+    core, row = row % ncore, row // ncore
+    y, row = row % ny, row // ny
+    x, row = row % nx, row // nx
+    zl, zh = row % nzl, row // nzl
+    places = (((zl * ncore + core) * nx + x) * nzh + zh) * ny + y
+    first_chan = (lax.axis_index(plane) * deep + lax.axis_index(ring)) * chan
     rate = lax.dynamic_slice_in_dim(decay_rate, first_chan, chan)
     gain = lax.dynamic_slice_in_dim(skip_gain, first_chan, chan)
     done = local_part(got, rate, gain, places, chan, cell, blocks * cell, interpret)
-    if two_stage:
-        done = done.reshape(seq_count, sub_count, 2, chan, cell)
-        far = jnp.transpose(lax.all_to_all(done, "seq", 0, 0), (1, 0, 2, 3, 4))
-        back = lax.all_to_all(far, "sub", 0, 0)
-    else:
-        back = lax.all_to_all(done.reshape(blocks, 2, chan, cell), both, 0, 0)
-    back = back.reshape(blocks, 2, chan, cell)
-    return tuple(
-        jnp.transpose(back[:, o].reshape(model_width, cell)) for o in range(2)
-    )
+    done = done.reshape(deep, flat, 2, chan, cell)
+    far = jnp.transpose(lax.all_to_all(done, ring, 0, 0), (1, 0, 2, 3, 4))
+    back = lax.all_to_all(far, plane, 0, 0).reshape(blocks, 2, chan, cell)
+    return tuple(jnp.transpose(back[:, o].reshape(model_width, cell)) for o in range(2))
 
 
 def solution(mesh, interpret=False):
+    side = round(mesh.shape["seq"] ** (1 / 3))
+    chips = mesh.devices.reshape(side, side, side, mesh.shape["sub"] // 2, 2)
+    fine = jax.sharding.Mesh(chips, ("x", "zh", "y", "zl", "core"))
+    split = P(tokens_over, None)
     return jax.shard_map(
         functools.partial(per_device, interpret=interpret),
-        mesh=mesh,
-        in_specs=(P(both, None), P(both, None), P(), P(), P(both, None)),
-        out_specs=(P(both, None), P(both, None)),
+        mesh=fine,
+        in_specs=(split, split, P(), P(), split),
+        out_specs=(split, split),
         check_vma=False,
     )

time: 171 us -> 156 us (0.912)
  blocking collectives: 90.9 us -> 53.9 us
  waiting for transfers between devices: 13.5 us -> 24.5 us
  starting transfers between devices: 16.1 us -> 23.4 us
  local copies, waits for them, and re-layouts: 17.9 us -> 21.1 us
    all_to_all x3 -> x2, blocking collectives: 90.9 us -> 53.9 us  [the longest x1 31.8 us: per_device(): far = jnp.transpose(lax.all_to_all(done, ring, 0, 0), (1, 0, 2, 3, 4))]
    all_to_all x1 -> x2, waiting for transfers between devices: 13.5 us -> 24.5 us  [the longest x1 13.6 us: per_device(): near = jnp.transpose(lax.all_to_all(leaving, plane, 0, 0), (1, 0, 2, 3, 4))]
    all_to_all x1 -> x2, starting transfers between devices: 16.1 us -> 23.4 us  [the longest x1 13 us: per_device(): got = lax.all_to_all(near, ring, 0, 0).reshape(blocks, 3 * chan * cell)]
    reshape x0 -> x3, local copies, waits for them, and re-layouts: none -> 2.53 us  [the longest x2 1.28 us: per_device(): done = done.reshape(deep, flat, 2, chan, cell)]
  transfers between devices with their start and end apart: 1 -> 2, of which waited for: 1 -> 2; matrix products, arithmetic and copies ran while one was open for 15% -> 17% of each run, Pallas kernels for 0% -> 0%
where the time goes in v2:
time: 156 us; the launch traced here: 155 us
  blocking collectives  53.9 us (35%)
  waiting for transfers between devices  24.5 us (16%)
  starting transfers between devices  23.4 us (15%)
  local copies, waits for them, and re-layouts  21.1 us (14%)
  other arithmetic  19.1 us (12%)
  Pallas kernels  11.1 us (7%)
  between operations  2.18 us (1%)
    all_to_all x1, blocking collectives, per_device(): far = jnp.transpose(lax.all_to_all(done, ring, 0, 0), (1, 0, 2, 3, 4))  31.8 us
    all_to_all x1, blocking collectives, per_device(): back = lax.all_to_all(far, plane, 0, 0).reshape(blocks, 2, chan, cell)  22 us
    all_to_all x1, waiting for transfers between devices, per_device(): near = jnp.transpose(lax.all_to_all(leaving, plane, 0, 0), (1, 0, 2, 3, 4))  13.6 us
    all_to_all x1, starting transfers between devices, per_device(): got = lax.all_to_all(near, ring, 0, 0).reshape(blocks, 3 * chan * cell)  13 us
    pallas_call x1, Pallas kernels, local_part(): pl.pallas_call(functools.partial(correlate, chan, cell, chunk, 2.0 / leng...  11.1 us
    all_to_all x1, waiting for transfers between devices, per_device(): got = lax.all_to_all(near, ring, 0, 0).reshape(blocks, 3 * chan * cell)  11 us
    all_to_all x1, starting transfers between devices, per_device(): near = jnp.transpose(lax.all_to_all(leaving, plane, 0, 0), (1, 0, 2, 3, 4))  10.4 us
    unnamed x5, local copies, waits for them, and re-layouts  5.06 us
  transfers between devices with their start and end apart: 2, of which 2 were waited for; matrix products, arithmetic and copies ran while one was open for 17% of the time, Pallas kernels for 0%

profile of v2, /device:TPU:1, one launch (start us, length us, event | category | flops | bytes accessed | tf_op | source)
XLA Modules:
  0.0 155.2 jit_solution(10901182292033427902)
XLA Ops:
  0.6 1.1 copy.32
  1.8 1.1 copy.33
  2.9 1.1 copy.34
  4.0 1.3 pad_maximum_fusion.2
  5.3 1.4 copy.35
  6.8 10.4 %all-to-all-start = ((bf16[32,16,3,2,128]{4,3,1,2,0:T(2,128)(2,1)}), bf16[32,16,3,2,128]{4,3,1,2,0:T(2,128)(2,1)S(1)}, u32[]{:S(2)}, u32[]{:S(2)}) async-start(bf16[32,16,3,2,128]{4,3,1,2,0:T(2,128)(2,1)} %copy.35), calls=%async_computation | async-start | bytes 1572864 | tf_op jit(solution)/shard_map/all_to_all | solution.py:190
  17.2 0.8 dynamic_slice.6
  18.0 13.6 %all-to-all-done = bf16[32,16,3,2,128]{4,3,1,2,0:T(2,128)(2,1)S(1)} async-done(((bf16[32,16,3,2,128]{4,3,1,2,0:T(2,128)(2,1)}), bf16[32,16,3,2,128]{4,3,1,2,0:T(2,128)(2,1)S(1)}, u32[]{:S(2)}, u32[]{:S(2)}) %all-to-all-start) | async-done | bytes 786464 | tf_op jit(solution)/shard_map/all_to_all | solution.py:190
  31.5 1.7 %copy.36 = bf16[16,32,3,2,128]{4,3,1,2,0:T(2,128)(2,1)} copy(bf16[16,32,3,2,128]{4,3,0,2,1:T(2,128)(2,1)S(1)} %bitcast.24) | data formatting | bytes 1572864 | tf_op jit(solution)/shard_map/transpose | solution.py:190
  33.3 13.0 %all-to-all-start.1 = ((bf16[16,32,3,2,128]{4,3,1,2,0:T(2,128)(2,1)}), bf16[16,32,3,2,128]{4,3,1,2,0:T(2,128)(2,1)S(1)}, u32[]{:S(2)}, u32[]{:S(2)}) async-start(bf16[16,32,3,2,128]{4,3,1,2,0:T(2,128)(2,1)} %copy.36), calls=%async_computation.1 | async-start | bytes 1572864 | tf_op jit(solution)/shard_map/all_to_all | solution.py:191
  46.3 0.6 fusion.54
  48.2 0.8 dynamic_slice.7
  49.0 4.2 %fusion.8 = (f32[512,4,1,128]{3,0,2,1:T(8,128)S(1)}, f32[512,4,1,128]{3,0,2,1:T(8,128)S(1)}) fusion(s32[4,128]{1,0:T(4,128)S(1)} %multiply_add_fusion.1, s32[512]{0:T(512)S(1)} %fusion.42), kind=kLoop, calls=%fused_computation.28 | loop fusion | flops 3932160 | bytes 2101248 | tf_op jit(solution)/shard_map/cos | solution.py:118
  53.2 0.1 pad_maximum_fusion.1
  53.4 2.9 %copy.38 = f32[512,4,2,128]{3,2,1,0:T(2,128)} copy(f32[512,4,2,128]{3,0,2,1:T(8,128)S(1)} %pad_maximum_fusion.1) | data formatting | bytes 4194304 | tf_op jit(solution)/shard_map/concatenate | solution.py:118
  56.3 3.1 %reshape.406 = f32[512,1024]{1,0:T(8,128)S(1)} reshape(f32[512,4,2,128]{3,2,1,0:T(2,128)} %copy.38) | data formatting | bytes 4194304 | tf_op jit(solution)/shard_map/reshape | solution.py:119
  59.5 0.3 fusion.30
  59.7 0.3 fusion.28
  60.0 1.5 exponential_multiply_fusion.1
  61.5 0.8 pad_maximum_fusion.3.env_ref
  62.3 0.8 fusion.13
  63.2 4.2 %fusion.9 = (f32[4,1,128,512]{3,2,1,0:T(8,128)S(1)}, f32[4,1,128,512]{3,2,1,0:T(8,128)S(1)}) fusion(s32[512]{0:T(512)S(1)} %fusion.42, s32[4,128]{1,0:T(4,128)S(1)} %multiply_add_fusion.1), kind=kLoop, calls=%fused_computation.29 | loop fusion | flops 3932160 | bytes 2101248 | tf_op jit(solution)/shard_map/cos | solution.py:115
  67.3 0.2 pad_maximum_fusion
  67.6 1.9 %fusion.20 = (f32[512,128]{1,0:T(8,128)}, f32[512,128]{1,0:T(8,128)}) fusion(s32[512]{0:T(512)S(1)} %multiply_add_fusion), kind=kLoop, calls=%fused_computation.54 | loop fusion | flops 917504 | bytes 526336 | tf_op jit(solution)/shard_map/sin | solution.py:172
  69.5 1.8 %fusion.1 = (bf16[512,1024]{1,0:T(8,128)(2,1)}, bf16[512,1024]{1,0:T(8,128)(2,1)}) fusion(f32[512,1024]{1,0:T(8,128)S(1)} %reshape.406), kind=kLoop, calls=%fused_computation.5 | loop fusion | flops 2097152 | bytes 4194304 | tf_op jit(solution)/shard_map/convert_element_type | solution.py:18
  71.3 1.7 %fusion = (bf16[1024,512]{1,0:T(8,128)(2,1)}, bf16[1024,512]{1,0:T(8,128)(2,1)}) fusion(f32[4,2,128,512]{3,2,1,0:T(8,128)S(1)} %pad_maximum_fusion), kind=kLoop, calls=%fused_computation.4 | loop fusion | flops 2097152 | bytes 4194304 | tf_op jit(solution)/shard_map/convert_element_type | solution.py:18
  72.9 11.0 %all-to-all-done.1 = bf16[16,32,3,2,128]{4,3,1,2,0:T(2,128)(2,1)S(1)} async-done(((bf16[16,32,3,2,128]{4,3,1,2,0:T(2,128)(2,1)}), bf16[16,32,3,2,128]{4,3,1,2,0:T(2,128)(2,1)S(1)}, u32[]{:S(2)}, u32[]{:S(2)}) %all-to-all-start.1) | async-done | bytes 786464 | tf_op jit(solution)/shard_map/all_to_all | solution.py:191
  83.9 0.6 copy.37
  84.5 1.3 reshape.404.got_ref
  85.7 0.6 broadcast_in_dim.2
  86.3 11.1 %shard_map.68 = bf16[512,512]{1,0:T(8,128)(2,1)} custom-call(bf16[512,768]{1,0:T(8,128)(2,1)} %reshape.404.got_ref, f32[512,256]{1,0:T(8,128)} %pad_maximum_fusion.3.env_ref, f32[1,256]{1,0:T(1,128)} %bitcast.32, bf16[1024,512]{1,0:T(8,128)(2,1)} %get-tuple-element.11.fwd_hi_ref, bf16[1024,512]{1,0:T(8,128)(2,1)} %get-tuple-element.10.fwd_lo_ref, ...), custom_call_target="tpu_custom_call" | custom-call | flops 6039797760 | bytes 8388608 | tf_op jit(solution)/shard_map/pallas_call | solution.py:143
  97.4 1.2 reshape.407
  98.6 0.1 copy.39
  98.7 31.8 %all_to_all.20 = bf16[16,32,2,2,128]{4,1,3,2,0:T(8,128)(2,1)S(1)} all-to-all(bf16[16,32,2,2,128]{4,1,3,2,0:T(8,128)(2,1)S(1)} %copy.39), channel_id=1, replica_groups=mesh['x'=4,'zh'=4,'y'=4,'zl'=4,'core'=2] {'zh','zl'}, dimensions={0} | all-to-all | bytes 1048576 | tf_op jit(solution)/shard_map/all_to_all | solution.py:203
  130.5 0.3 copy.40
  130.8 22.0 %all_to_all.21 = bf16[32,16,2,2,128]{4,1,3,2,0:T(8,128)(2,1)S(1)} all-to-all(bf16[32,16,2,2,128]{4,1,3,2,0:T(8,128)(2,1)S(1)} %copy.40), channel_id=1, replica_groups=mesh['x'=4,'zh'=4,'y'=4,'zl'=4,'core'=2] {'x','y','core'}, dimensions={0} | all-to-all | bytes 1048576 | tf_op jit(solution)/shard_map/all_to_all | solution.py:204
  153.0 0.3 copy.42
  153.3 0.9 copy.44
  154.1 0.3 copy.43
  154.4 0.9 copy.45
  (6 shorter events, 0.1 us)
Async XLA Ops:
  6.8 24.8 %all-to-all-start = ((bf16[32,16,3,2,128]{4,3,1,2,0:T(2,128)(2,1)}), bf16[32,16,3,2,128]{4,3,1,2,0:T(2,128)(2,1)S(1)}, u32[]{:S(2)}, u32[]{:S(2)}) async-start(bf16[32,16,3,2,128]{4,3,1,2,0:T(2,128)(2,1)} %copy.35), calls=%async_computation | async-start | bytes 1572864 | tf_op jit(solution)/shard_map/all_to_all | solution.py:190
  33.3 50.6 %all-to-all-start.1 = ((bf16[16,32,3,2,128]{4,3,1,2,0:T(2,128)(2,1)}), bf16[16,32,3,2,128]{4,3,1,2,0:T(2,128)(2,1)S(1)}, u32[]{:S(2)}, u32[]{:S(2)}) async-start(bf16[16,32,3,2,128]{4,3,1,2,0:T(2,128)(2,1)} %copy.36), calls=%async_computation.1 | async-start | bytes 1572864 | tf_op jit(solution)/shard_map/all_to_all | solution.py:191

commit v3 on v2

v3 whole, which is shorter than its diff:
```python
import functools
import math

import jax
import jax.numpy as jnp
import numpy as np
from jax import lax
from jax.experimental import pallas as pl
from jax.experimental.pallas import tpu as pltpu
from jax.sharding import PartitionSpec as P

tokens_over = ("zl", "core", "x", "zh", "y")
plane = ("x", "y", "core")
ring = ("zh", "zl")


def table(values):
    high = values.astype(jnp.bfloat16)
    low = (values - high.astype(np.float64)).astype(jnp.bfloat16)
    return high, low


def halves(values):
    high = values.astype(jnp.bfloat16)
    return high, (values - high.astype(jnp.float32)).astype(jnp.bfloat16)


def mul(left, right):
    return jnp.dot(left, right, preferred_element_type=jnp.float32)


def mul_left(left, right):
    dims = (((0,), (0,)), ((), ()))
    return lax.dot_general(left, right, dims, preferred_element_type=jnp.float32)


def mul3(left, right):
    left_hi, left_lo = left
    right_hi, right_lo = right
    return mul(left_hi, right_hi) + (mul(left_hi, right_lo) + mul(left_lo, right_hi))


def correlate(
    chan, cell, chunk, scale,
    up_ref, raw_ref, act_ref, env_ref, gain_ref, fwd_hi_ref, fwd_lo_ref,
    inner_hi_ref, inner_lo_ref, outer_hi_ref, outer_lo_ref, cos_ref, sin_ref,
    through_ref, across_ref, taps_hi_ref, taps_lo_ref, total_ref,
):
    step = pl.program_id(0)
    width = chan * cell

    @pl.when(step == 0)
    def _():
        taps = raw_ref[...].astype(jnp.float32) * env_ref[...]
        high, low = halves(taps)
        taps_hi_ref[...] = high
        taps_lo_ref[...] = low
        total_ref[...] = jnp.zeros_like(total_ref)

    fwd_hi = fwd_hi_ref[...]
    fwd_lo = fwd_lo_ref[...]
    act = act_ref[...]
    up = up_ref[...]
    first = (
        mul(fwd_hi, act) + mul(fwd_lo, act),
        mul(fwd_hi, taps_hi_ref[...])
        + (mul(fwd_hi, taps_lo_ref[...]) + mul(fwd_lo, taps_hi_ref[...])),
        mul(fwd_hi, up) + mul(fwd_lo, up),
    )
    cosine = cos_ref[...]
    sine = sin_ref[...]
    inner = (inner_hi_ref[...], inner_lo_ref[...])
    outer = (outer_hi_ref[...], outer_lo_ref[...])
    spectra = []
    for values in first:
        rows = []
        for c in range(chan):
            re = values[:chunk, c * cell : (c + 1) * cell]
            im = values[chunk:, c * cell : (c + 1) * cell]
            rows.append(
                jnp.concatenate([re * cosine + im * sine, im * cosine - re * sine], axis=1)
            )
        spectra.append(mul3(halves(jnp.concatenate(rows, axis=0)), inner))
    up_re, up_im = spectra[2][:, :cell], spectra[2][:, cell:]
    parts_re, parts_im = [], []
    for other in (spectra[1], spectra[0]):
        re, im = other[:, :cell], other[:, cell:]
        mixed = jnp.concatenate([up_re * re + up_im * im, up_im * re - up_re * im], axis=1)
        back = mul3(halves(mixed), outer)
        for c in range(chan):
            zre = back[c * chunk : (c + 1) * chunk, :cell]
            zim = back[c * chunk : (c + 1) * chunk, cell:]
            parts_re.append(zre * cosine - zim * sine)
            parts_im.append(zim * cosine + zre * sine)
    spread = jnp.concatenate(
        [jnp.concatenate(parts_re, axis=1), jnp.concatenate(parts_im, axis=1)], axis=0
    )
    spread_hi, spread_lo = halves(spread)
    total_ref[...] += mul_left(fwd_hi, spread_hi) + (
        mul_left(fwd_hi, spread_lo) + mul_left(fwd_lo, spread_hi)
    )

    @pl.when(step == pl.num_programs(0) - 1)
    def _():
        through = total_ref[:, :width] * scale
        across = total_ref[:, width:] * scale
        up_float = up_ref[...].astype(jnp.float32)
        through_ref[...] = (through + gain_ref[...] * up_float).astype(jnp.bfloat16)
        across_ref[...] = (across * env_ref[...]).astype(jnp.bfloat16)


def local_part(up, raw, act, rate, gain, places, cell, total_tokens, interpret=False):
    blocks, width = up.shape
    chan = width // cell
    chunk = min(128, blocks)
    steps = blocks // chunk
    length = 2 * total_tokens
    odd = 2 * np.arange(blocks) + 1
    turns = 2.0 * math.pi * (odd[:, None] * places[None, :] % (4 * blocks)) / (4 * blocks)
    turns = turns.reshape(steps, 1, chunk, blocks)
    fwd = np.concatenate([np.cos(turns), -np.sin(turns)], 1).reshape(2 * blocks, blocks)
    fwd_hi, fwd_lo = table(fwd)
    cells = np.arange(cell)
    turns = 2.0 * math.pi * (cells[:, None] * cells[None, :] % cell) / cell
    inner = np.block([[np.cos(turns), -np.sin(turns)], [np.sin(turns), np.cos(turns)]])
    inner_hi, inner_lo = table(inner)
    outer_hi, outer_lo = table(inner.T)
    turns = 2.0 * math.pi * (odd[:, None] * cells[None, :]) / (2 * length)
    at = jnp.asarray(places[:, None] * cell + cells[None, :], jnp.float32)
    env = jnp.concatenate(
        [
            jnp.sqrt(2.0 * rate[c] / total_tokens) * jnp.exp(-(rate[c] * at) / total_tokens)
            for c in range(chan)
        ],
        1,
    )
    gain_row = jnp.repeat(gain, cell)[None, :]
    whole = lambda shape: pl.BlockSpec(shape, lambda i: (0, 0))
    flops = 2 * 3 * (5 * 2 * blocks * blocks * width + 5 * chan * blocks * 4 * cell * cell)
    return pl.pallas_call(
        functools.partial(correlate, chan, cell, chunk, 2.0 / length),
        grid=(steps,),
        out_shape=[jax.ShapeDtypeStruct((blocks, width), jnp.bfloat16)] * 2,
        in_specs=[whole((blocks, width))] * 4
        + [
            whole((1, width)),
            pl.BlockSpec((2 * chunk, blocks), lambda i: (i, 0)),
            pl.BlockSpec((2 * chunk, blocks), lambda i: (i, 0)),
        ]
        + [whole((2 * cell, 2 * cell))] * 4
        + [pl.BlockSpec((chunk, cell), lambda i: (i, 0))] * 2,
        out_specs=[whole((blocks, width))] * 2,
        scratch_shapes=[
            pltpu.VMEM((blocks, width), jnp.bfloat16),
            pltpu.VMEM((blocks, width), jnp.bfloat16),
            pltpu.VMEM((blocks, 2 * width), jnp.float32),
        ],
        cost_estimate=pl.CostEstimate(flops=flops, bytes_accessed=8 * 2**20, transcendentals=0),
        interpret=interpret,
    )(
        up, raw, act, env, gain_row, fwd_hi, fwd_lo, inner_hi, inner_lo, outer_hi, outer_lo,
        np.cos(turns).astype(np.float32), np.sin(turns).astype(np.float32),
    )


def place_of(names, sizes):
    at = 0
    for name in names:
        at = at * sizes[name] + lax.axis_index(name)
    return at


def device_at(names, sizes, at):
    where = {}
    for name in reversed(names):
        where[name] = lax.rem(at, sizes[name])
        at = lax.div(at, sizes[name])
    return where


def exchange_kernel(count, near, far, sizes, *refs):
    source, result, middle = refs[:count], refs[count : 2 * count], refs[2 * count : 3 * count]
    near_send, near_recv, far_send, far_recv, own = refs[3 * count :]
    near_count, far_count = source[0].shape[:2]
    near_at, far_at = place_of(near, sizes), place_of(far, sizes)
    barrier = pltpu.get_barrier_semaphore()

    def greet(names, at, total):
        def one(k, carry):
            peer = device_at(names, sizes, lax.rem(at + k, total))
            pl.semaphore_signal(
                barrier, inc=1, device_id=peer, device_id_type=pl.DeviceIdType.MESH
            )
            return carry

        lax.fori_loop(1, total, one, 0)

    greet(near, near_at, near_count)
    greet(far, far_at, far_count)
    pl.semaphore_wait(barrier, near_count + far_count - 2)

    def spread(names, at, total, piece, landing, send_sem, recv_sem):
        def one(k, carry):
            ahead = lax.div(k + 1, 2)
            to = lax.rem(at + jnp.where(lax.rem(k, 2) == 1, ahead, total - ahead), total)
            pltpu.make_async_remote_copy(
                src_ref=piece(to),
                dst_ref=landing,
                send_sem=send_sem,
                recv_sem=recv_sem,
                device_id=device_at(names, sizes, to),
                device_id_type=pl.DeviceIdType.MESH,
            ).start()
            return carry

        lax.fori_loop(1, total, one, 0)

    own_copies = []
    for i in range(count):
        spread(
            near, near_at, near_count, lambda to: source[i].at[to],
            middle[i].at[near_at], near_send.at[i], near_recv.at[i],
        )
        copy = pltpu.make_async_copy(source[i].at[near_at], middle[i].at[near_at], own.at[i])
        copy.start()
        own_copies.append(copy)
    for i in range(count):
        others = middle[i].at[pl.ds(0, near_count - 1)]
        pltpu.make_async_copy(others, others, near_recv.at[i]).wait()
        own_copies[i].wait()
        spread(
            far, far_at, far_count, lambda to: middle[i].at[:, to],
            result[i].at[far_at], far_send.at[i], far_recv.at[i],
        )
        copy = pltpu.make_async_copy(middle[i].at[:, far_at], result[i].at[far_at], own.at[i])
        copy.start()
        own_copies[i] = copy
    for i in range(count):
        own_copies[i].wait()
        others = source[i].at[pl.ds(0, near_count - 1)]
        pltpu.make_async_copy(others, others, near_send.at[i]).wait()
        others = result[i].at[pl.ds(0, far_count - 1)]
        pltpu.make_async_copy(others, others, far_send.at[i]).wait()
        pltpu.make_async_copy(others, others, far_recv.at[i]).wait()


def exchange(arrays, near, far, sizes, number, interpret):
    count = len(arrays)
    near_count, far_count, chan, cell = arrays[0].shape
    one = jax.ShapeDtypeStruct((far_count, near_count, chan, cell), arrays[0].dtype)
    return pl.pallas_call(
        functools.partial(exchange_kernel, count, near, far, sizes),
        out_shape=[one] * count,
        in_specs=[pl.BlockSpec(memory_space=pltpu.VMEM)] * count,
        out_specs=[pl.BlockSpec(memory_space=pltpu.VMEM)] * count,
        scratch_shapes=[pltpu.VMEM(arrays[0].shape, arrays[0].dtype)] * count
        + [pltpu.SemaphoreType.DMA((count,))] * 5,
        compiler_params=pltpu.CompilerParams(collective_id=number, has_side_effects=True),
        interpret=interpret,
    )(*arrays)


def per_device(sizes, activation, filter_raw, decay_rate, skip_gain, grad_out, interpret=False):
    cell, model_width = activation.shape
    flat = math.prod(sizes[n] for n in plane)
    deep = math.prod(sizes[n] for n in ring)
    blocks = flat * deep
    chan = model_width // blocks
    leaving = [
        jnp.transpose(v).reshape(flat, deep, chan, cell)
        for v in (grad_out, filter_raw, activation)
    ]
    got = exchange(leaving, plane, ring, sizes, 0, interpret and pltpu.InterpretParams())
    row = np.arange(blocks)
    at = {}
    for name in reversed(ring + plane):
        at[name] = row % sizes[name]
        row = row // sizes[name]
    places = 0
    for name in tokens_over:
        places = places * sizes[name] + at[name]
    first_chan = (lax.axis_index(plane) * deep + lax.axis_index(ring)) * chan
    rate = lax.dynamic_slice_in_dim(decay_rate, first_chan, chan)
    gain = lax.dynamic_slice_in_dim(skip_gain, first_chan, chan)
    up, raw, act = (v.reshape(blocks, chan * cell) for v in got)
    done = local_part(up, raw, act, rate, gain, places, cell, blocks * cell, bool(interpret))
    done = [v.reshape(deep, flat, chan, cell) for v in done]
    back = exchange(done, ring, plane, sizes, 1, interpret and pltpu.InterpretParams())
    return tuple(jnp.transpose(v.reshape(model_width, cell)) for v in back)


def solution(mesh, interpret=False):
    side = round(mesh.shape["seq"] ** (1 / 3))
    chips = mesh.devices.reshape(side, side, side, mesh.shape["sub"] // 2, 2)
    fine = jax.sharding.Mesh(chips, ("x", "zh", "y", "zl", "core"))
    split = P(tokens_over, None)
    return jax.shard_map(
        functools.partial(per_device, dict(fine.shape), interpret=interpret),
        mesh=fine,
        in_specs=(split, split, P(), P(), split),
        out_specs=(split, split),
        check_vma=False,
    )
```

time: 156 us -> 138 us (0.88)
  Pallas kernels: 11.1 us -> 119 us
  blocking collectives: 53.9 us -> 0 us
  waiting for transfers between devices: 24.5 us -> 0 us
  starting transfers between devices: 23.4 us -> 0 us
  other arithmetic: 19.1 us -> 2.18 us
  local copies, waits for them, and re-layouts: 21.1 us -> 14.3 us
    pallas_call x0 -> x2, Pallas kernels: none -> 108 us  [exchange(): pl.pallas_call(functools.partial(exchange_kernel, count, near, far, sizes...]
    all_to_all x2 -> x0, blocking collectives: 53.9 us -> none  [the longest x1 31.8 us: per_device(): far = jnp.transpose(lax.all_to_all(done, ring, 0, 0), (1, 0, 2, 3, 4))]
    all_to_all x2 -> x0, waiting for transfers between devices: 24.5 us -> none  [the longest x1 13.6 us: per_device(): near = jnp.transpose(lax.all_to_all(leaving, plane, 0, 0), (1, 0, 2, 3, 4))]
    all_to_all x2 -> x0, starting transfers between devices: 23.4 us -> none  [the longest x1 13 us: per_device(): got = lax.all_to_all(near, ring, 0, 0).reshape(blocks, 3 * chan * cell)]
    cos x2 -> x0, other arithmetic: 8.34 us -> none  [the longest x1 4.18 us: local_part(): fwd = jnp.concatenate([jnp.cos(fwd_angle), -jnp.sin(fwd_angle)], 1)]
    convert_element_type x3 -> x0, other arithmetic: 4.24 us -> none  [split_halves(): return (high.astype(jnp.bfloat16), (values - high).astype(jnp.bfloat16))]
    unnamed x5 -> x15, local copies, waits for them, and re-layouts: 5.06 us -> 1.97 us
    concatenate x1 -> x0, local copies, waits for them, and re-layouts: 2.94 us -> none  [local_part(): back = jnp.concatenate([jnp.cos(back_angle), -jnp.sin(back_angle)], 2)]
  transfers between devices with their start and end apart: 2 -> 0, of which waited for: 2 -> 0; matrix products, arithmetic and copies ran while one was open for 17% -> 0% of each run, Pallas kernels for 0% -> 0%
where the time goes in v3:
time: 138 us; the launch traced here: 137 us
  Pallas kernels  119 us (86%)
  local copies, waits for them, and re-layouts  14.3 us (10%)
  other arithmetic  2.18 us (2%)
  between operations  2.06 us (1%)
    pallas_call x2, Pallas kernels, exchange(): pl.pallas_call(functools.partial(exchange_kernel, count, near, far, sizes...  108 us
    pallas_call x1, Pallas kernels, local_part(): pl.pallas_call(functools.partial(correlate, chan, cell, chunk, 2.0 / leng...  10.8 us
    transpose x3, local copies, waits for them, and re-layouts, per_device(): jnp.transpose(v).reshape(flat, deep, chan, cell)  3.52 us

profile of v3, /device:TPU:1, one launch (start us, length us, event | category | flops | bytes accessed | tf_op | source)
XLA Modules:
  0.0 137.2 jit_solution(6343385442903060792)
XLA Ops:
  0.6 0.8 dynamic_slice.6
  1.4 0.8 dynamic_slice.7
  2.2 0.6 broadcast_in_dim.3
  2.8 0.6 fusion
  4.7 0.0 copy-start.1
  4.7 1.8 %copy.18 = bf16[1024,128]{1,0:T(8,128)(2,1)} copy(bf16[1024,128]{0,1:T(8,128)(2,1)} %bitcast.29) | data formatting | bytes 524288 | tf_op jit(solution)/shard_map/transpose | solution.py:270
  6.6 0.0 copy-done.1
  6.6 0.0 copy-start.2
  6.6 0.8 copy.17
  7.4 0.1 copy-done.2
  7.5 0.8 copy.16
  8.4 60.8 %shard_map.149 = (bf16[16,32,2,128]{3,2,1,0:T(2,128)(2,1)}, bf16[16,32,2,128]{3,2,1,0:T(2,128)(2,1)}, bf16[16,32,2,128]{3,2,1,0:T(2,128)(2,1)}) custom-call(bf16[32,16,2,128]{3,2,1,0:T(2,128)(2,1)} %bitcast.28, bf16[32,16,2,128]{3,2,1,0:T(2,128)(2,1)} %bitcast.27, bf16[32,16,2,128]{3,2,1,0:T(2,128)(2,1)} %bitcast.26), custom_call_target="tpu_custom_call" | custom-call | tf_op jit(solution)/shard_map/pallas_call | solution.py:251
  69.2 0.0 copy-start.5
  69.2 0.0 copy-start.6
  69.2 1.7 %copy.27 = bf16[64,8,2,128]{3,1,2,0:T(8,128)(2,1)} copy(bf16[64,8,2,128]{3,2,1,0:T(2,128)(2,1)} %bitcast.35) | data formatting | bytes 524288
  71.0 0.0 copy-done.5
  71.0 0.0 copy-done.6
  71.0 0.0 copy-start
  71.0 0.8 copy_bitcast_fusion
  71.8 0.1 copy-done
  71.9 1.3 exponential_multiply_fusion.1
  73.3 0.8 pad_maximum_fusion.env_ref
  74.1 10.8 %shard_map.150 = (bf16[512,256]{1,0:T(8,128)(2,1)}, bf16[512,256]{1,0:T(8,128)(2,1)}) custom-call(bf16[512,256]{1,0:T(8,128)(2,1)} %bitcast.32, bf16[512,256]{1,0:T(8,128)(2,1)} %get-tuple-element.21.raw_ref, bf16[512,256]{1,0:T(8,128)(2,1)} %get-tuple-element.20.act_ref, f32[512,256]{1,0:T(8,128)} %pad_maximum_fusion.env_ref, f32[1,256]{1,0:T(1,128)} %bitcast.40, ...), custom_call_target="tpu_custom_call" | custom-call | flops 6039797760 | bytes 8388608 | tf_op jit(solution)/shard_map/pallas_call | solution.py:140
  85.0 0.0 copy-start.3
  85.0 1.8 %reshape.40.refs_0_ = bf16[16,32,2,128]{3,2,1,0:T(2,128)(2,1)} reshape(bf16[512,256]{1,0:T(8,128)(2,1)} %get-tuple-element.12) | data formatting | bytes 524288 | tf_op jit(solution)/shard_map/reshape | solution.py:287
  86.7 0.0 copy-done.3
  86.7 0.8 reshape.41.refs_1_
  87.5 47.0 %shard_map.151 = (bf16[32,16,2,128]{3,2,1,0:T(2,128)(2,1)}, bf16[32,16,2,128]{3,2,1,0:T(2,128)(2,1)}) custom-call(bf16[16,32,2,128]{3,2,1,0:T(2,128)(2,1)} %reshape.40.refs_0_, bf16[16,32,2,128]{3,2,1,0:T(2,128)(2,1)} %reshape.41.refs_1_), custom_call_target="tpu_custom_call" | custom-call | tf_op jit(solution)/shard_map/pallas_call | solution.py:251
  134.5 0.0 copy-start.4
  134.5 1.8 %copy.19 = bf16[1024,128]{0,1:T(8,128)(2,1)} copy(bf16[1024,128]{1,0:T(8,128)(2,1)} %bitcast.37) | data formatting | bytes 524288 | tf_op jit(solution)/shard_map/reshape | solution.py:289
  136.3 0.0 copy-done.4
  136.3 0.8 copy.20
Async XLA Ops:
  4.7 1.9 %copy-start.1 = (bf16[128,1024]{1,0:T(8,128)(2,1)S(1)}, bf16[128,1024]{1,0:T(8,128)(2,1)}, u32[]{:S(2)}) copy-start(bf16[128,1024]{1,0:T(8,128)(2,1)} %param.15) | copy-start | bytes 786436
  6.6 1.0 copy-start.2
  69.2 1.8 %copy-start.5 = (bf16[16,32,2,128]{3,2,1,0:T(2,128)(2,1)S(1)}, bf16[16,32,2,128]{3,2,1,0:T(2,128)(2,1)}, u32[]{:S(2)}) copy-start(bf16[16,32,2,128]{3,2,1,0:T(2,128)(2,1)} %get-tuple-element.10) | copy-start | bytes 786436
  69.2 1.8 %copy-start.6 = (bf16[16,32,2,128]{3,2,1,0:T(2,128)(2,1)S(1)}, bf16[16,32,2,128]{3,2,1,0:T(2,128)(2,1)}, u32[]{:S(2)}) copy-start(bf16[16,32,2,128]{3,2,1,0:T(2,128)(2,1)} %get-tuple-element.11) | copy-start | bytes 786436
  71.0 1.0 copy-start
  85.0 1.8 %copy-start.3 = (bf16[512,256]{1,0:T(8,128)(2,1)S(1)}, bf16[512,256]{1,0:T(8,128)(2,1)}, u32[]{:S(2)}) copy-start(bf16[512,256]{1,0:T(8,128)(2,1)} %get-tuple-element.13) | copy-start | bytes 786436
  134.5 1.8 %copy-start.4 = (bf16[32,16,2,128]{3,2,1,0:T(2,128)(2,1)S(1)}, bf16[32,16,2,128]{3,2,1,0:T(2,128)(2,1)}, u32[]{:S(2)}) copy-start(bf16[32,16,2,128]{3,2,1,0:T(2,128)(2,1)} %get-tuple-element.15) | copy-start | bytes 786436

commit v4 on v2

v4 whole, which is shorter than its diff:
```python
import functools
import math

import jax
import jax.numpy as jnp
import numpy as np
from jax import lax
from jax.experimental import pallas as pl
from jax.experimental.pallas import tpu as pltpu
from jax.sharding import PartitionSpec as P

tokens_over = ("zl", "core", "x", "zh", "y")
plane = ("x", "y", "core")
ring = ("zh", "zl")


def table(values):
    high = values.astype(jnp.bfloat16)
    low = (values - high.astype(np.float64)).astype(jnp.bfloat16)
    return high, low


def halves(values):
    high = values.astype(jnp.bfloat16)
    return high, (values - high.astype(jnp.float32)).astype(jnp.bfloat16)


def mul(left, right):
    return jnp.dot(left, right, preferred_element_type=jnp.float32)


def mul_left(left, right):
    dims = (((0,), (0,)), ((), ()))
    return lax.dot_general(left, right, dims, preferred_element_type=jnp.float32)


def mul3(left, right):
    left_hi, left_lo = left
    right_hi, right_lo = right
    return mul(left_hi, right_hi) + (mul(left_hi, right_lo) + mul(left_lo, right_hi))


def place_of(names, sizes):
    at = 0
    for name in names:
        at = at * sizes[name] + lax.axis_index(name)
    return at


def device_at(names, sizes, at):
    where = {}
    for name in reversed(names):
        where[name] = lax.rem(at, sizes[name])
        at = lax.div(at, sizes[name])
    return where


def fused_kernel(
    sizes, chunk,
    up_ref, raw_ref, act_ref, rate_ref, gain_ref, at_ref, fwd_hi_ref, fwd_lo_ref,
    inner_hi_ref, inner_lo_ref, outer_hi_ref, outer_lo_ref, cos_ref, sin_ref,
    through_ref, across_ref,
    mid_up, mid_raw, mid_act, got_up, got_raw, got_act, done_through, done_across,
    mid_through, mid_across, spec_ref, total_ref, env_ref, taps_hi_ref, taps_lo_ref,
    flat_send, flat_recv, deep_send, deep_recv, flat_own, deep_own,
):
    flat, deep, chan, cell = up_ref.shape
    blocks, width = flat * deep, chan * cell
    steps = blocks // chunk
    tokens = blocks * cell
    flat_at, deep_at = place_of(plane, sizes), place_of(ring, sizes)
    barrier = pltpu.get_barrier_semaphore()
    mesh_id = pl.DeviceIdType.MESH

    def greet(names, at, count):
        def one(k, carry):
            peer = device_at(names, sizes, lax.rem(at + k, count))
            pl.semaphore_signal(barrier, inc=1, device_id=peer, device_id_type=mesh_id)
            return carry

        lax.fori_loop(1, count, one, 0)

    greet(plane, flat_at, flat)
    greet(ring, deep_at, deep)
    pl.semaphore_wait(barrier, flat + deep - 2)

    def spread(names, at, count, piece, landing, send_sem, recv_sem, own_sem):
        def one(k, carry):
            ahead = lax.div(k + 1, 2)
            to = lax.rem(at + jnp.where(lax.rem(k, 2) == 1, ahead, count - ahead), count)
            pltpu.make_async_remote_copy(
                src_ref=piece(to),
                dst_ref=landing,
                send_sem=send_sem,
                recv_sem=recv_sem,
                device_id=device_at(names, sizes, to),
                device_id_type=mesh_id,
            ).start()
            return carry

        lax.fori_loop(1, count, one, 0)
        own = pltpu.make_async_copy(piece(at), landing, own_sem)
        own.start()
        return own

    def settle(ref, count, sem):
        others = ref.at[pl.ds(0, count - 1)]
        pltpu.make_async_copy(others, others, sem).wait()

    def over_plane(i, piece, landing):
        return spread(
            plane, flat_at, flat, piece, landing, flat_send.at[i], flat_recv.at[i], flat_own.at[i]
        )

    def over_ring(i, piece, landing):
        return spread(
            ring, deep_at, deep, piece, landing, deep_send.at[i], deep_recv.at[i], deep_own.at[i]
        )

    leaving = (up_ref, raw_ref, act_ref)
    middle = (mid_up, mid_raw, mid_act)
    got = (got_up, got_raw, got_act)
    own_flat = [
        over_plane(i, lambda to: leaving[i].at[to], middle[i].at[flat_at]) for i in range(3)
    ]
    first_chan = (flat_at * deep + deep_at) * chan
    at = at_ref[...]
    for c in range(chan):
        rate = jnp.full((1, cell), rate_ref[first_chan + c], jnp.float32)
        env_ref[:, c * cell : (c + 1) * cell] = jnp.sqrt(2.0 * rate / tokens) * jnp.exp(
            -(rate * at) / tokens
        )
    own_deep = []
    for i in range(3):
        settle(middle[i], flat, flat_recv.at[i])
        own_flat[i].wait()
        own_deep.append(
            over_ring(i, lambda to: middle[i].at[:, to], got[i].at[deep_at])
        )

    inner = (inner_hi_ref[...], inner_lo_ref[...])
    outer = (outer_hi_ref[...], outer_lo_ref[...])

    def arrived(i):
        settle(got[i], deep, deep_recv.at[i])
        own_deep[i].wait()
        return got[i][...].reshape(blocks, width)

    def tables(s):
        rows = pl.ds(pl.multiple_of(s * 2 * chunk, 2 * chunk), 2 * chunk)
        few = pl.ds(pl.multiple_of(s * chunk, chunk), chunk)
        return fwd_hi_ref[rows, :], fwd_lo_ref[rows, :], cos_ref[few, :], sin_ref[few, :]

    def forward(values, cosine, sine):
        rows = []
        for c in range(chan):
            re = values[:chunk, c * cell : (c + 1) * cell]
            im = values[chunk:, c * cell : (c + 1) * cell]
            rows.append(
                jnp.concatenate([re * cosine + im * sine, im * cosine - re * sine], axis=1)
            )
        return mul3(halves(jnp.concatenate(rows, axis=0)), inner)

    def inverse(s, other, fwd_hi, fwd_lo, cosine, sine):
        ahead = spec_ref[s]
        up_re, up_im = ahead[:, :cell], ahead[:, cell:]
        re, im = other[:, :cell], other[:, cell:]
        mixed = jnp.concatenate([up_re * re + up_im * im, up_im * re - up_re * im], axis=1)
        back = mul3(halves(mixed), outer)
        parts_re, parts_im = [], []
        for c in range(chan):
            zre = back[c * chunk : (c + 1) * chunk, :cell]
            zim = back[c * chunk : (c + 1) * chunk, cell:]
            parts_re.append(zre * cosine - zim * sine)
            parts_im.append(zim * cosine + zre * sine)
        spread_hi, spread_lo = halves(
            jnp.concatenate(
                [jnp.concatenate(parts_re, axis=1), jnp.concatenate(parts_im, axis=1)], axis=0
            )
        )
        total_ref[...] += mul_left(fwd_hi, spread_hi) + (
            mul_left(fwd_hi, spread_lo) + mul_left(fwd_lo, spread_hi)
        )

    taps_hi_ref[...] = arrived(0)

    def up_step(s, carry):
        fwd_hi, fwd_lo, cosine, sine = tables(s)
        up = taps_hi_ref[...]
        spec_ref[s] = forward(mul(fwd_hi, up) + mul(fwd_lo, up), cosine, sine)
        return carry

    lax.fori_loop(0, steps, up_step, 0)

    taps_hi, taps_lo = halves(arrived(1).astype(jnp.float32) * env_ref[...])
    taps_hi_ref[...] = taps_hi
    taps_lo_ref[...] = taps_lo
    total_ref[...] = jnp.zeros_like(total_ref)

    def taps_step(s, carry):
        fwd_hi, fwd_lo, cosine, sine = tables(s)
        high = taps_hi_ref[...]
        first = mul(fwd_hi, high) + (mul(fwd_hi, taps_lo_ref[...]) + mul(fwd_lo, high))
        inverse(s, forward(first, cosine, sine), fwd_hi, fwd_lo, cosine, sine)
        return carry

    lax.fori_loop(0, steps, taps_step, 0)
    scale = 1.0 / tokens
    up_float = got_up[...].reshape(blocks, width).astype(jnp.float32)
    gain = jnp.concatenate(
        [jnp.full((1, cell), gain_ref[first_chan + c], jnp.float32) for c in range(chan)], axis=1
    )
    through = (total_ref[...] * scale + gain * up_float).astype(jnp.bfloat16)
    done_through[...] = through.reshape(done_through.shape)
    own_deep.append(
        over_ring(3, lambda to: done_through.at[to], mid_through.at[deep_at])
    )

    taps_hi_ref[...] = arrived(2)
    total_ref[...] = jnp.zeros_like(total_ref)

    def act_step(s, carry):
        fwd_hi, fwd_lo, cosine, sine = tables(s)
        act = taps_hi_ref[...]
        first = mul(fwd_hi, act) + mul(fwd_lo, act)
        inverse(s, forward(first, cosine, sine), fwd_hi, fwd_lo, cosine, sine)
        return carry

    lax.fori_loop(0, steps, act_step, 0)
    across = (total_ref[...] * scale * env_ref[...]).astype(jnp.bfloat16)
    done_across[...] = across.reshape(done_across.shape)
    own_deep.append(
        over_ring(4, lambda to: done_across.at[to], mid_across.at[deep_at])
    )
    leaving = leaving + (done_through, done_across)
    middle = middle + (mid_through, mid_across)
    final = (through_ref, across_ref)
    for i in range(2):
        settle(middle[3 + i], deep, deep_recv.at[3 + i])
        own_deep[3 + i].wait()
        own_flat.append(
            over_plane(3 + i, lambda to: middle[3 + i].at[:, to], final[i].at[flat_at])
        )
    for i in range(3):
        settle(leaving[i], flat, flat_send.at[i])
        settle(got[i], deep, deep_send.at[i])
    for i in range(2):
        settle(done_through, deep, deep_send.at[3 + i])
        settle(final[i], flat, flat_send.at[3 + i])
        settle(final[i], flat, flat_recv.at[3 + i])
        own_flat[3 + i].wait()


def fused(leaving, decay_rate, skip_gain, places, sizes, interpret):
    flat, deep, chan, cell = leaving[0].shape
    blocks, width = flat * deep, chan * cell
    chunk = min(128, blocks)
    steps = blocks // chunk
    length = 2 * blocks * cell
    odd = 2 * np.arange(blocks) + 1
    turns = 2.0 * math.pi * (odd[:, None] * places[None, :] % (4 * blocks)) / (4 * blocks)
    turns = turns.reshape(steps, 1, chunk, blocks)
    fwd = np.concatenate([np.cos(turns), -np.sin(turns)], 1).reshape(2 * blocks, blocks)
    fwd_hi, fwd_lo = table(fwd)
    cells = np.arange(cell)
    turns = 2.0 * math.pi * (cells[:, None] * cells[None, :] % cell) / cell
    inner = np.block([[np.cos(turns), -np.sin(turns)], [np.sin(turns), np.cos(turns)]])
    inner_hi, inner_lo = table(inner)
    outer_hi, outer_lo = table(inner.T)
    turns = 2.0 * math.pi * (odd[:, None] * cells[None, :]) / (2 * length)
    at = (places[:, None] * cell + cells[None, :]).astype(np.float32)
    near = pltpu.VMEM((flat, deep, chan, cell), jnp.bfloat16)
    far = pltpu.VMEM((deep, flat, chan, cell), jnp.bfloat16)
    vmem = pl.BlockSpec(memory_space=pltpu.VMEM)
    smem = pl.BlockSpec(memory_space=pltpu.SMEM)
    return pl.pallas_call(
        functools.partial(fused_kernel, sizes, chunk),
        out_shape=[jax.ShapeDtypeStruct(leaving[0].shape, jnp.bfloat16)] * 2,
        in_specs=[vmem] * 3 + [smem] * 2 + [vmem] * 9,
        out_specs=[vmem] * 2,
        scratch_shapes=[near] * 3
        + [far] * 7
        + [
            pltpu.VMEM((steps, chan * chunk, 2 * cell), jnp.float32),
            pltpu.VMEM((blocks, width), jnp.float32),
            pltpu.VMEM((blocks, width), jnp.float32),
            pltpu.VMEM((blocks, width), jnp.bfloat16),
            pltpu.VMEM((blocks, width), jnp.bfloat16),
        ]
        + [pltpu.SemaphoreType.DMA((5,))] * 6,
        compiler_params=pltpu.CompilerParams(collective_id=0, has_side_effects=True),
        interpret=interpret,
    )(
        *leaving, decay_rate, skip_gain, at, fwd_hi, fwd_lo, inner_hi, inner_lo, outer_hi,
        outer_lo, np.cos(turns).astype(np.float32), np.sin(turns).astype(np.float32),
    )


def per_device(sizes, activation, filter_raw, decay_rate, skip_gain, grad_out, interpret=False):
    cell, model_width = activation.shape
    flat = math.prod(sizes[n] for n in plane)
    deep = math.prod(sizes[n] for n in ring)
    blocks = flat * deep
    chan = model_width // blocks
    leaving = [
        jnp.transpose(v).reshape(flat, deep, chan, cell)
        for v in (grad_out, filter_raw, activation)
    ]
    row = np.arange(blocks)
    at = {}
    for name in reversed(ring + plane):
        at[name] = row % sizes[name]
        row = row // sizes[name]
    places = 0
    for name in tokens_over:
        places = places * sizes[name] + at[name]
    back = fused(
        leaving, decay_rate, skip_gain, places, sizes, interpret and pltpu.InterpretParams()
    )
    return tuple(jnp.transpose(v.reshape(model_width, cell)) for v in back)


def solution(mesh, interpret=False):
    side = round(mesh.shape["seq"] ** (1 / 3))
    chips = mesh.devices.reshape(side, side, side, mesh.shape["sub"] // 2, 2)
    fine = jax.sharding.Mesh(chips, ("x", "zh", "y", "zl", "core"))
    split = P(tokens_over, None)
    return jax.shard_map(
        functools.partial(per_device, dict(fine.shape), interpret=interpret),
        mesh=fine,
        in_specs=(split, split, P(), P(), split),
        out_specs=(split, split),
        check_vma=False,
    )
```

time: 156 us -> 103 us (0.66)
  Pallas kernels: 11.1 us -> 95.5 us
  blocking collectives: 53.9 us -> 0 us
  waiting for transfers between devices: 24.5 us -> 0 us
  starting transfers between devices: 23.4 us -> 0 us
  other arithmetic: 19.1 us -> 0 us
  local copies, waits for them, and re-layouts: 21.1 us -> 6.3 us
    pallas_call x1, Pallas kernels: 11.1 us -> 95.5 us  [fused(): pl.pallas_call(functools.partial(fused_kernel, sizes, chunk), out_shape=[...]
    all_to_all x2 -> x0, blocking collectives: 53.9 us -> none  [the longest x1 31.8 us: per_device(): far = jnp.transpose(lax.all_to_all(done, ring, 0, 0), (1, 0, 2, 3, 4))]
    all_to_all x2 -> x0, waiting for transfers between devices: 24.5 us -> none  [the longest x1 13.6 us: per_device(): near = jnp.transpose(lax.all_to_all(leaving, plane, 0, 0), (1, 0, 2, 3, 4))]
    all_to_all x2 -> x0, starting transfers between devices: 23.4 us -> none  [the longest x1 13 us: per_device(): got = lax.all_to_all(near, ring, 0, 0).reshape(blocks, 3 * chan * cell)]
    cos x2 -> x0, other arithmetic: 8.34 us -> none  [the longest x1 4.18 us: local_part(): fwd = jnp.concatenate([jnp.cos(fwd_angle), -jnp.sin(fwd_angle)], 1)]
    unnamed x5 -> x6, local copies, waits for them, and re-layouts: 5.06 us -> 0.12 us
    convert_element_type x3 -> x0, other arithmetic: 4.24 us -> none  [split_halves(): return (high.astype(jnp.bfloat16), (values - high).astype(jnp.bfloat16))]
    reshape x4 -> x2, local copies, waits for them, and re-layouts: 5.64 us -> 2.68 us  [per_device(): return tuple((jnp.transpose(v.reshape(model_width, cell)) for v in back))]
  transfers between devices with their start and end apart: 2 -> 0, of which waited for: 2 -> 0; matrix products, arithmetic and copies ran while one was open for 17% -> 0% of each run, Pallas kernels for 0% -> 0%
where the time goes in v4:
time: 103 us; the launch traced here: 102 us
  Pallas kernels  95.5 us (93%)
  local copies, waits for them, and re-layouts  6.3 us (6%)
    pallas_call x1, Pallas kernels, fused(): pl.pallas_call(functools.partial(fused_kernel, sizes, chunk), out_shape=[...  95.5 us
    transpose x3, local copies, waits for them, and re-layouts, per_device(): jnp.transpose(v).reshape(flat, deep, chan, cell)  3.5 us
    reshape x2, local copies, waits for them, and re-layouts, per_device(): return tuple((jnp.transpose(v.reshape(model_width, cell)) for v in back))  2.68 us

profile of v4, /device:TPU:1, one launch (start us, length us, event | category | flops | bytes accessed | tf_op | source)
XLA Modules:
  0.0 102.4 jit_solution(14205928087549675931)
XLA Ops:
  0.6 0.0 copy-start
  0.6 1.8 %copy.18 = bf16[1024,128]{1,0:T(8,128)(2,1)} copy(bf16[1024,128]{0,1:T(8,128)(2,1)} %bitcast.13) | data formatting | bytes 524288 | tf_op jit(solution)/shard_map/transpose | solution.py:306
  2.5 0.0 copy-done
  2.5 0.0 copy-start.1
  2.5 0.8 copy.17
  3.3 0.1 copy-done.1
  3.4 0.8 copy.16
  4.3 95.5 %shard_map.149 = (bf16[32,16,2,128]{3,2,1,0:T(2,128)(2,1)}, bf16[32,16,2,128]{3,2,1,0:T(2,128)(2,1)}) custom-call(bf16[32,16,2,128]{3,2,1,0:T(2,128)(2,1)} %bitcast.12, bf16[32,16,2,128]{3,2,1,0:T(2,128)(2,1)} %bitcast.11, bf16[32,16,2,128]{3,2,1,0:T(2,128)(2,1)} %bitcast.10, f32[1024]{0:T(1024)} %rate_ref.1, f32[1024]{0:T(1024)} %gain_ref.1, ...), custom_call_target="tpu_custom_call" | custom-call | tf_op jit(solution)/shard_map/pallas_call | solution.py:276
  99.7 0.0 copy-start.2
  99.7 1.8 %copy.19 = bf16[1024,128]{0,1:T(8,128)(2,1)} copy(bf16[1024,128]{1,0:T(8,128)(2,1)} %bitcast.17) | data formatting | bytes 524288 | tf_op jit(solution)/shard_map/reshape | solution.py:320
  101.6 0.0 copy-done.2
  101.6 0.8 copy.20
Async XLA Ops:
  0.6 1.8 %copy-start = (bf16[128,1024]{1,0:T(8,128)(2,1)S(1)}, bf16[128,1024]{1,0:T(8,128)(2,1)}, u32[]{:S(2)}) copy-start(bf16[128,1024]{1,0:T(8,128)(2,1)} %param.15) | copy-start | bytes 786436
  2.5 1.0 copy-start.1
  99.7 1.8 %copy-start.2 = (bf16[32,16,2,128]{3,2,1,0:T(2,128)(2,1)S(1)}, bf16[32,16,2,128]{3,2,1,0:T(2,128)(2,1)}, u32[]{:S(2)}) copy-start(bf16[32,16,2,128]{3,2,1,0:T(2,128)(2,1)} %get-tuple-element.5) | copy-start | bytes 786436

commit v5 on v4

--- a/solution.py
+++ b/solution.py
@@ -10,8 +10,8 @@
 from jax.sharding import PartitionSpec as P
 
 tokens_over = ("zl", "core", "x", "zh", "y")
-plane = ("x", "y", "core")
-ring = ("zh", "zl")
+plane = ("core", "x", "y")
+ring = ("zl", "zh")
 
 
 def table(values):
@@ -57,14 +57,14 @@
 
 def fused_kernel(
     sizes, chunk,
-    up_ref, raw_ref, act_ref, rate_ref, gain_ref, at_ref, fwd_hi_ref, fwd_lo_ref,
+    up_ref, raw_ref, act_ref, rate_ref, gain_ref, at_ref, fwd_hi_far, fwd_lo_far,
     inner_hi_ref, inner_lo_ref, outer_hi_ref, outer_lo_ref, cos_ref, sin_ref,
     through_ref, across_ref,
-    mid_up, mid_raw, mid_act, got_up, got_raw, got_act, done_through, done_across,
+    out_up, out_raw, out_act, mid_up, mid_raw, mid_act, got_up, got_raw, got_act, done_through, done_across,
     mid_through, mid_across, spec_ref, total_ref, env_ref, taps_hi_ref, taps_lo_ref,
-    flat_send, flat_recv, deep_send, deep_recv, flat_own, deep_own,
+    fwd_hi_ref, fwd_lo_ref, flat_send, flat_recv, deep_send, deep_recv, held_sem,
 ):
-    flat, deep, chan, cell = up_ref.shape
+    flat, deep, chan, cell = out_up.shape
     blocks, width = flat * deep, chan * cell
     steps = blocks // chunk
     tokens = blocks * cell
@@ -82,47 +82,69 @@
 
     greet(plane, flat_at, flat)
     greet(ring, deep_at, deep)
+    held = [
+        pltpu.make_async_copy(fwd_hi_far, fwd_hi_ref, held_sem.at[0]),
+        pltpu.make_async_copy(fwd_lo_far, fwd_lo_ref, held_sem.at[1]),
+    ]
+    for copy in held:
+        copy.start()
+    for given, turned in ((up_ref, out_up), (raw_ref, out_raw), (act_ref, out_act)):
+        turned[...] = jnp.transpose(given[...]).reshape(turned.shape)
     pl.semaphore_wait(barrier, flat + deep - 2)
 
-    def spread(names, at, count, piece, landing, send_sem, recv_sem, own_sem):
+    parts = (2, 1, 1, 1, 2)
+
+    def spread(names, at, low, count, piece, landing, send_sem, recv_sem):
         def one(k, carry):
-            ahead = lax.div(k + 1, 2)
-            to = lax.rem(at + jnp.where(lax.rem(k, 2) == 1, ahead, count - ahead), count)
-            pltpu.make_async_remote_copy(
-                src_ref=piece(to),
-                dst_ref=landing,
-                send_sem=send_sem,
-                recv_sem=recv_sem,
-                device_id=device_at(names, sizes, to),
-                device_id_type=mesh_id,
-            ).start()
+            to = low + lax.rem(at + k, count)
+
+            @pl.when(to != at)
+            def _():
+                pltpu.make_async_remote_copy(
+                    src_ref=piece(to),
+                    dst_ref=landing,
+                    send_sem=send_sem,
+                    recv_sem=recv_sem,
+                    device_id=device_at(names, sizes, to),
+                    device_id_type=mesh_id,
+                ).start()
+
+            @pl.when(to == at)
+            def _():
+                pltpu.make_async_copy(piece(at), landing, recv_sem).start()
+
             return carry
 
-        lax.fori_loop(1, count, one, 0)
-        own = pltpu.make_async_copy(piece(at), landing, own_sem)
-        own.start()
-        return own
-
-    def settle(ref, count, sem):
-        others = ref.at[pl.ds(0, count - 1)]
-        pltpu.make_async_copy(others, others, sem).wait()
-
-    def over_plane(i, piece, landing):
-        return spread(
-            plane, flat_at, flat, piece, landing, flat_send.at[i], flat_recv.at[i], flat_own.at[i]
-        )
-
-    def over_ring(i, piece, landing):
-        return spread(
-            ring, deep_at, deep, piece, landing, deep_send.at[i], deep_recv.at[i], deep_own.at[i]
-        )
-
-    leaving = (up_ref, raw_ref, act_ref)
-    middle = (mid_up, mid_raw, mid_act)
-    got = (got_up, got_raw, got_act)
-    own_flat = [
-        over_plane(i, lambda to: leaving[i].at[to], middle[i].at[flat_at]) for i in range(3)
-    ]
+        lax.fori_loop(1, count + 1, one, 0)
+
+    def settle(ref, sem):
+        pltpu.make_async_copy(ref, ref, sem).wait()
+
+    def cut(i, h, count):
+        return pl.ds(h * (count // parts[i]), count // parts[i])
+
+    def first_stage(i, names, at, count, other, send_sem, recv_sem):
+        for h in range(parts[i]):
+            rows = cut(i, h, other)
+            spread(
+                names, at, 0, count, lambda to: leaving[i].at[to, rows],
+                middle[i].at[at, rows], send_sem.at[i], recv_sem.at[i, h],
+            )
+
+    def second_stage(i, names, at, count, waited, send_sem, recv_sem):
+        for h in range(parts[i]):
+            settle(middle[i].at[:, cut(i, h, count)], waited.at[i, h])
+            size = count // parts[i]
+            spread(
+                names, at, h * size, size, lambda to: middle[i].at[:, to],
+                landed[i].at[at], send_sem.at[i], recv_sem.at[i, 0],
+            )
+
+    leaving = (out_up, out_raw, out_act, done_through, done_across)
+    middle = (mid_up, mid_raw, mid_act, mid_through, mid_across)
+    landed = (got_up, got_raw, got_act, through_ref, across_ref)
+    for i in range(3):
+        first_stage(i, plane, flat_at, flat, deep, flat_send, flat_recv)
     first_chan = (flat_at * deep + deep_at) * chan
     at = at_ref[...]
     for c in range(chan):
@@ -130,21 +152,17 @@
         env_ref[:, c * cell : (c + 1) * cell] = jnp.sqrt(2.0 * rate / tokens) * jnp.exp(
             -(rate * at) / tokens
         )
-    own_deep = []
     for i in range(3):
-        settle(middle[i], flat, flat_recv.at[i])
-        own_flat[i].wait()
-        own_deep.append(
-            over_ring(i, lambda to: middle[i].at[:, to], got[i].at[deep_at])
-        )
+        second_stage(i, ring, deep_at, deep, flat_recv, deep_send, deep_recv)
+    for copy in held:
+        copy.wait()
 
     inner = (inner_hi_ref[...], inner_lo_ref[...])
     outer = (outer_hi_ref[...], outer_lo_ref[...])
 
     def arrived(i):
-        settle(got[i], deep, deep_recv.at[i])
-        own_deep[i].wait()
-        return got[i][...].reshape(blocks, width)
+        settle(landed[i], deep_recv.at[i, 0])
+        return landed[i][...].reshape(blocks, width)
 
     def tables(s):
         rows = pl.ds(pl.multiple_of(s * 2 * chunk, 2 * chunk), 2 * chunk)
@@ -212,9 +230,7 @@
     )
     through = (total_ref[...] * scale + gain * up_float).astype(jnp.bfloat16)
     done_through[...] = through.reshape(done_through.shape)
-    own_deep.append(
-        over_ring(3, lambda to: done_through.at[to], mid_through.at[deep_at])
-    )
+    first_stage(3, ring, deep_at, deep, flat, deep_send, deep_recv)
 
     taps_hi_ref[...] = arrived(2)
     total_ref[...] = jnp.zeros_like(total_ref)
@@ -229,30 +245,20 @@
     lax.fori_loop(0, steps, act_step, 0)
     across = (total_ref[...] * scale * env_ref[...]).astype(jnp.bfloat16)
     done_across[...] = across.reshape(done_across.shape)
-    own_deep.append(
-        over_ring(4, lambda to: done_across.at[to], mid_across.at[deep_at])
-    )
-    leaving = leaving + (done_through, done_across)
-    middle = middle + (mid_through, mid_across)
-    final = (through_ref, across_ref)
-    for i in range(2):
-        settle(middle[3 + i], deep, deep_recv.at[3 + i])
-        own_deep[3 + i].wait()
-        own_flat.append(
-            over_plane(3 + i, lambda to: middle[3 + i].at[:, to], final[i].at[flat_at])
-        )
-    for i in range(3):
-        settle(leaving[i], flat, flat_send.at[i])
-        settle(got[i], deep, deep_send.at[i])
-    for i in range(2):
-        settle(done_through, deep, deep_send.at[3 + i])
-        settle(final[i], flat, flat_send.at[3 + i])
-        settle(final[i], flat, flat_recv.at[3 + i])
-        own_flat[3 + i].wait()
-
-
-def fused(leaving, decay_rate, skip_gain, places, sizes, interpret):
-    flat, deep, chan, cell = leaving[0].shape
+    first_stage(4, ring, deep_at, deep, flat, deep_send, deep_recv)
+    for i in (3, 4):
+        second_stage(i, plane, flat_at, flat, deep_recv, flat_send, flat_recv)
+    for i in range(5):
+        first_send, last_send = (flat_send, deep_send) if i < 3 else (deep_send, flat_send)
+        settle(leaving[i].at[pl.ds(0, leaving[i].shape[0] - 1)], first_send.at[i])
+        settle(landed[i].at[pl.ds(0, landed[i].shape[0] - 1)], last_send.at[i])
+    for i in (3, 4):
+        settle(landed[i], flat_recv.at[i, 0])
+
+
+def fused(given, decay_rate, skip_gain, places, flat, deep, sizes, interpret):
+    cell = given[0].shape[0]
+    chan = given[0].shape[1] // (flat * deep)
     blocks, width = flat * deep, chan * cell
     chunk = min(128, blocks)
     steps = blocks // chunk
@@ -275,10 +281,10 @@
     smem = pl.BlockSpec(memory_space=pltpu.SMEM)
     return pl.pallas_call(
         functools.partial(fused_kernel, sizes, chunk),
-        out_shape=[jax.ShapeDtypeStruct(leaving[0].shape, jnp.bfloat16)] * 2,
-        in_specs=[vmem] * 3 + [smem] * 2 + [vmem] * 9,
+        out_shape=[jax.ShapeDtypeStruct((flat, deep, chan, cell), jnp.bfloat16)] * 2,
+        in_specs=[vmem] * 3 + [smem] * 2 + [vmem] + [pl.BlockSpec(memory_space=pl.ANY)] * 2 + [vmem] * 6,
         out_specs=[vmem] * 2,
-        scratch_shapes=[near] * 3
+        scratch_shapes=[near] * 6
         + [far] * 7
         + [
             pltpu.VMEM((steps, chan * chunk, 2 * cell), jnp.float32),
@@ -286,12 +292,15 @@
             pltpu.VMEM((blocks, width), jnp.float32),
             pltpu.VMEM((blocks, width), jnp.bfloat16),
             pltpu.VMEM((blocks, width), jnp.bfloat16),
+            pltpu.VMEM((2 * blocks, blocks), jnp.bfloat16),
+            pltpu.VMEM((2 * blocks, blocks), jnp.bfloat16),
         ]
-        + [pltpu.SemaphoreType.DMA((5,))] * 6,
+        + [pltpu.SemaphoreType.DMA((5,)), pltpu.SemaphoreType.DMA((5, 2))] * 2
+        + [pltpu.SemaphoreType.DMA((2,))],
         compiler_params=pltpu.CompilerParams(collective_id=0, has_side_effects=True),
         interpret=interpret,
     )(
-        *leaving, decay_rate, skip_gain, at, fwd_hi, fwd_lo, inner_hi, inner_lo, outer_hi,
+        *given, decay_rate, skip_gain, at, fwd_hi, fwd_lo, inner_hi, inner_lo, outer_hi,
         outer_lo, np.cos(turns).astype(np.float32), np.sin(turns).astype(np.float32),
     )
 
@@ -301,11 +310,6 @@
     flat = math.prod(sizes[n] for n in plane)
     deep = math.prod(sizes[n] for n in ring)
     blocks = flat * deep
-    chan = model_width // blocks
-    leaving = [
-        jnp.transpose(v).reshape(flat, deep, chan, cell)
-        for v in (grad_out, filter_raw, activation)
-    ]
     row = np.arange(blocks)
     at = {}
     for name in reversed(ring + plane):
@@ -315,7 +319,8 @@
     for name in tokens_over:
         places = places * sizes[name] + at[name]
     back = fused(
-        leaving, decay_rate, skip_gain, places, sizes, interpret and pltpu.InterpretParams()
+        (grad_out, filter_raw, activation), decay_rate, skip_gain, places, flat, deep, sizes,
+        interpret and pltpu.InterpretParams(),
     )
     return tuple(jnp.transpose(v.reshape(model_width, cell)) for v in back)
 

time: 103 us -> 95.7 us (0.929)
  local copies, waits for them, and re-layouts: 6.3 us -> 2.69 us
  Pallas kernels: 95.5 us -> 92.2 us
    transpose x3 -> x0, local copies, waits for them, and re-layouts: 3.5 us -> none  [per_device(): jnp.transpose(v).reshape(flat, deep, chan, cell)]
    pallas_call x1, Pallas kernels: 95.5 us -> 92.2 us  [fused(): pl.pallas_call(functools.partial(fused_kernel, sizes, chunk), out_shape=[...]
where the time goes in v5:
time: 95.7 us; the launch traced here: 95.6 us
  Pallas kernels  92.2 us (96%)
  local copies, waits for them, and re-layouts  2.69 us (3%)
    pallas_call x1, Pallas kernels, fused(): pl.pallas_call(functools.partial(fused_kernel, sizes, chunk), out_shape=[...  92.2 us
    reshape x2, local copies, waits for them, and re-layouts, per_device(): return tuple((jnp.transpose(v.reshape(model_width, cell)) for v in back))  2.68 us

profile of v5, /device:TPU:1, one launch (start us, length us, event | category | flops | bytes accessed | tf_op | source)
XLA Modules:
  0.0 95.6 jit_solution(12105152758761919813)
XLA Ops:
  0.6 92.2 %shard_map.149 = (bf16[32,16,2,128]{3,2,1,0:T(2,128)(2,1)}, bf16[32,16,2,128]{3,2,1,0:T(2,128)(2,1)}) custom-call(bf16[128,1024]{1,0:T(8,128)(2,1)} %up_ref.1, bf16[128,1024]{1,0:T(8,128)(2,1)} %raw_ref.1, bf16[128,1024]{1,0:T(8,128)(2,1)} %act_ref.1, f32[1024]{0:T(1024)} %rate_ref.1, f32[1024]{0:T(1024)} %gain_ref.1, f32[512,128]{1,0:T(8,128)} %constant.18.clone.at_ref, ...), custom_call_target="tpu_custom_call" | custom-call | tf_op jit(solution)/shard_map/pallas_call | solution.py:282
  92.9 0.0 copy-start
  92.9 1.8 %copy.16 = bf16[1024,128]{0,1:T(8,128)(2,1)} copy(bf16[1024,128]{1,0:T(8,128)(2,1)} %bitcast.5) | data formatting | bytes 524288 | tf_op jit(solution)/shard_map/reshape | solution.py:325
  94.7 0.0 copy-done
  94.7 0.8 copy.17
Async XLA Ops:
  92.9 1.8 %copy-start = (bf16[32,16,2,128]{3,2,1,0:T(2,128)(2,1)S(1)}, bf16[32,16,2,128]{3,2,1,0:T(2,128)(2,1)}, u32[]{:S(2)}) copy-start(bf16[32,16,2,128]{3,2,1,0:T(2,128)(2,1)} %get-tuple-element.5) | copy-start | bytes 786436

commit v6 on v5

--- a/solution.py
+++ b/solution.py
@@ -92,7 +92,9 @@
         turned[...] = jnp.transpose(given[...]).reshape(turned.shape)
     pl.semaphore_wait(barrier, flat + deep - 2)
 
-    parts = (2, 1, 1, 1, 2)
+    halves_x = 2 - sizes["x"] % 2
+    parts = (sizes["zl"], 1, 1, 1, 2 * halves_x)
+    half_at = lax.div(lax.axis_index("x"), sizes["x"] // halves_x)
 
     def spread(names, at, low, count, piece, landing, send_sem, recv_sem):
         def one(k, carry):
@@ -121,11 +123,19 @@
         pltpu.make_async_copy(ref, ref, sem).wait()
 
     def cut(i, h, count):
-        return pl.ds(h * (count // parts[i]), count // parts[i])
+        size = count // parts[i]
+        slot = 0
+        if i == 0:
+            slot = lax.rem(lax.axis_index("zl") + h, sizes["zl"])
+        if i == 4:
+            core = lax.rem(lax.axis_index("core") + 1 - h // halves_x, 2)
+            half = lax.rem(half_at + halves_x - 1 - h % halves_x, halves_x)
+            slot = core * halves_x + half
+        return slot * size, size
 
     def first_stage(i, names, at, count, other, send_sem, recv_sem):
         for h in range(parts[i]):
-            rows = cut(i, h, other)
+            rows = pl.ds(*cut(i, h, other))
             spread(
                 names, at, 0, count, lambda to: leaving[i].at[to, rows],
                 middle[i].at[at, rows], send_sem.at[i], recv_sem.at[i, h],
@@ -133,18 +143,26 @@
 
     def second_stage(i, names, at, count, waited, send_sem, recv_sem):
         for h in range(parts[i]):
-            settle(middle[i].at[:, cut(i, h, count)], waited.at[i, h])
-            size = count // parts[i]
+            low, size = cut(i, h, count)
+            settle(middle[i].at[:, pl.ds(low, size)], waited.at[i, h])
             spread(
-                names, at, h * size, size, lambda to: middle[i].at[:, to],
+                names, at, low, size, lambda to: middle[i].at[:, to],
                 landed[i].at[at], send_sem.at[i], recv_sem.at[i, 0],
             )
 
     leaving = (out_up, out_raw, out_act, done_through, done_across)
     middle = (mid_up, mid_raw, mid_act, mid_through, mid_across)
     landed = (got_up, got_raw, got_act, through_ref, across_ref)
-    for i in range(3):
+    def leave(i):
         first_stage(i, plane, flat_at, flat, deep, flat_send, flat_recv)
+
+    def pass_on(i):
+        second_stage(i, ring, deep_at, deep, flat_recv, deep_send, deep_recv)
+
+    leave(0)
+    leave(1)
+    pass_on(0)
+    leave(2)
     first_chan = (flat_at * deep + deep_at) * chan
     at = at_ref[...]
     for c in range(chan):
@@ -152,8 +170,8 @@
         env_ref[:, c * cell : (c + 1) * cell] = jnp.sqrt(2.0 * rate / tokens) * jnp.exp(
             -(rate * at) / tokens
         )
-    for i in range(3):
-        second_stage(i, ring, deep_at, deep, flat_recv, deep_send, deep_recv)
+    pass_on(1)
+    pass_on(2)
     for copy in held:
         copy.wait()
 
@@ -295,7 +313,7 @@
             pltpu.VMEM((2 * blocks, blocks), jnp.bfloat16),
             pltpu.VMEM((2 * blocks, blocks), jnp.bfloat16),
         ]
-        + [pltpu.SemaphoreType.DMA((5,)), pltpu.SemaphoreType.DMA((5, 2))] * 2
+        + [pltpu.SemaphoreType.DMA((5,)), pltpu.SemaphoreType.DMA((5, max(4, sizes["zl"])))] * 2
         + [pltpu.SemaphoreType.DMA((2,))],
         compiler_params=pltpu.CompilerParams(collective_id=0, has_side_effects=True),
         interpret=interpret,

time: 95.7 us -> 93.7 us (0.979)
  Pallas kernels: 92.2 us -> 89.8 us
    pallas_call x1, Pallas kernels: 92.2 us -> 89.8 us  [fused(): pl.pallas_call(functools.partial(fused_kernel, sizes, chunk), out_shape=[...]
where the time goes in v6:
time: 93.7 us; the launch traced here: 93.2 us
  Pallas kernels  89.8 us (96%)
  local copies, waits for them, and re-layouts  2.69 us (3%)
    pallas_call x1, Pallas kernels, fused(): pl.pallas_call(functools.partial(fused_kernel, sizes, chunk), out_shape=[...  89.8 us
    reshape x2, local copies, waits for them, and re-layouts, per_device(): return tuple((jnp.transpose(v.reshape(model_width, cell)) for v in back))  2.68 us

profile of v6, /device:TPU:1, one launch (start us, length us, event | category | flops | bytes accessed | tf_op | source)
XLA Modules:
  0.0 93.2 jit_solution(15999696756932062834)
XLA Ops:
  0.6 89.8 %shard_map.149 = (bf16[32,16,2,128]{3,2,1,0:T(2,128)(2,1)}, bf16[32,16,2,128]{3,2,1,0:T(2,128)(2,1)}) custom-call(bf16[128,1024]{1,0:T(8,128)(2,1)} %up_ref.1, bf16[128,1024]{1,0:T(8,128)(2,1)} %raw_ref.1, bf16[128,1024]{1,0:T(8,128)(2,1)} %act_ref.1, f32[1024]{0:T(1024)} %rate_ref.1, f32[1024]{0:T(1024)} %gain_ref.1, f32[512,128]{1,0:T(8,128)} %constant.18.clone.at_ref, ...), custom_call_target="tpu_custom_call" | custom-call | tf_op jit(solution)/shard_map/pallas_call | solution.py:300
  90.5 0.0 copy-start
  90.5 1.8 %copy.16 = bf16[1024,128]{0,1:T(8,128)(2,1)} copy(bf16[1024,128]{1,0:T(8,128)(2,1)} %bitcast.5) | data formatting | bytes 524288 | tf_op jit(solution)/shard_map/reshape | solution.py:343
  92.3 0.0 copy-done
  92.3 0.8 copy.17
Async XLA Ops:
  90.5 1.8 %copy-start = (bf16[32,16,2,128]{3,2,1,0:T(2,128)(2,1)S(1)}, bf16[32,16,2,128]{3,2,1,0:T(2,128)(2,1)}, u32[]{:S(2)}) copy-start(bf16[32,16,2,128]{3,2,1,0:T(2,128)(2,1)} %get-tuple-element.5) | copy-start | bytes 786436

commit v7 on v6

--- a/solution.py
+++ b/solution.py
@@ -62,7 +62,7 @@
     through_ref, across_ref,
     out_up, out_raw, out_act, mid_up, mid_raw, mid_act, got_up, got_raw, got_act, done_through, done_across,
     mid_through, mid_across, spec_ref, total_ref, env_ref, taps_hi_ref, taps_lo_ref,
-    fwd_hi_ref, fwd_lo_ref, flat_send, flat_recv, deep_send, deep_recv, held_sem,
+    fwd_hi_ref, fwd_lo_ref, early, flat_send, flat_recv, deep_send, deep_recv, held_sem,
 ):
     flat, deep, chan, cell = out_up.shape
     blocks, width = flat * deep, chan * cell
@@ -159,10 +159,21 @@
     def pass_on(i):
         second_stage(i, ring, deep_at, deep, flat_recv, deep_send, deep_recv)
 
+    groups, size = sizes["zl"], sizes["zh"]
+    zl_at, zh_at = lax.axis_index("zl"), lax.axis_index("zh")
+    spread(
+        ring, deep_at, zl_at * size, size, lambda to: out_act.at[:, to],
+        early.at[zh_at], deep_send.at[2], deep_recv.at[2, 1],
+    )
     leave(0)
     leave(1)
     pass_on(0)
-    leave(2)
+    for h in range(1, groups):
+        rows = pl.ds(lax.rem(zl_at + h, groups) * size, size)
+        spread(
+            plane, flat_at, 0, flat, lambda to: out_act.at[to, rows],
+            mid_act.at[flat_at, rows], flat_send.at[2], flat_recv.at[2, h - 1],
+        )
     first_chan = (flat_at * deep + deep_at) * chan
     at = at_ref[...]
     for c in range(chan):
@@ -171,7 +182,19 @@
             -(rate * at) / tokens
         )
     pass_on(1)
-    pass_on(2)
+    for h in range(1, groups):
+        low = lax.rem(zl_at + h, groups) * size
+        settle(mid_act.at[:, pl.ds(low, size)], flat_recv.at[2, h - 1])
+        spread(
+            ring, deep_at, low, size, lambda to: mid_act.at[:, to],
+            got_act.at[deep_at], deep_send.at[2], deep_recv.at[2, 0],
+        )
+    own_rows = pl.ds(zl_at * size, size)
+    settle(early, deep_recv.at[2, 1])
+    spread(
+        plane, flat_at, 0, flat, lambda to: early.at[:, to],
+        got_act.at[own_rows, flat_at], flat_send.at[2], flat_recv.at[2, groups - 1],
+    )
     for copy in held:
         copy.wait()
 
@@ -179,7 +202,12 @@
     outer = (outer_hi_ref[...], outer_lo_ref[...])
 
     def arrived(i):
-        settle(landed[i], deep_recv.at[i, 0])
+        if i < 2:
+            settle(landed[i], deep_recv.at[i, 0])
+        else:
+            if groups > 1:
+                settle(got_act.at[pl.ds(0, deep - size)], deep_recv.at[2, 0])
+            settle(got_act.at[own_rows], flat_recv.at[2, groups - 1])
         return landed[i][...].reshape(blocks, width)
 
     def tables(s):
@@ -312,6 +340,7 @@
             pltpu.VMEM((blocks, width), jnp.bfloat16),
             pltpu.VMEM((2 * blocks, blocks), jnp.bfloat16),
             pltpu.VMEM((2 * blocks, blocks), jnp.bfloat16),
+            pltpu.VMEM((sizes["zh"], flat, chan, cell), jnp.bfloat16),
         ]
         + [pltpu.SemaphoreType.DMA((5,)), pltpu.SemaphoreType.DMA((5, max(4, sizes["zl"])))] * 2
         + [pltpu.SemaphoreType.DMA((2,))],

time: 93.7 us -> 93.6 us (level)
  no operation moved by 1% of the time
where the time goes in v7:
time: 93.6 us; the launch traced here: 92.5 us
  Pallas kernels  89.2 us (95%)
  local copies, waits for them, and re-layouts  2.69 us (3%)
    pallas_call x1, Pallas kernels, fused(): pl.pallas_call(functools.partial(fused_kernel, sizes, chunk), out_shape=[...  89.2 us
    reshape x2, local copies, waits for them, and re-layouts, per_device(): return tuple((jnp.transpose(v.reshape(model_width, cell)) for v in back))  2.68 us

profile of v7, /device:TPU:1, one launch (start us, length us, event | category | flops | bytes accessed | tf_op | source)
XLA Modules:
  0.0 92.5 jit_solution(3551738984943689076)
XLA Ops:
  0.6 89.2 %shard_map.149 = (bf16[32,16,2,128]{3,2,1,0:T(2,128)(2,1)}, bf16[32,16,2,128]{3,2,1,0:T(2,128)(2,1)}) custom-call(bf16[128,1024]{1,0:T(8,128)(2,1)} %up_ref.1, bf16[128,1024]{1,0:T(8,128)(2,1)} %raw_ref.1, bf16[128,1024]{1,0:T(8,128)(2,1)} %act_ref.1, f32[1024]{0:T(1024)} %rate_ref.1, f32[1024]{0:T(1024)} %gain_ref.1, f32[512,128]{1,0:T(8,128)} %constant.18.clone.at_ref, ...), custom_call_target="tpu_custom_call" | custom-call | tf_op jit(solution)/shard_map/pallas_call | solution.py:328
  89.8 0.0 copy-start
  89.8 1.8 %copy.16 = bf16[1024,128]{0,1:T(8,128)(2,1)} copy(bf16[1024,128]{1,0:T(8,128)(2,1)} %bitcast.5) | data formatting | bytes 524288 | tf_op jit(solution)/shard_map/reshape | solution.py:372
  91.7 0.0 copy-done
  91.7 0.8 copy.17
Async XLA Ops:
  89.8 1.8 %copy-start = (bf16[32,16,2,128]{3,2,1,0:T(2,128)(2,1)S(1)}, bf16[32,16,2,128]{3,2,1,0:T(2,128)(2,1)}, u32[]{:S(2)}) copy-start(bf16[32,16,2,128]{3,2,1,0:T(2,128)(2,1)} %get-tuple-element.5) | copy-start | bytes 786436
